TPU v7x, 256 devices: a whole 4x4x8 slice. The times are simulated.
256 devices in a mesh: ctx: 32 (over z, x), head: 8 (over y, core).
Axes of the slice: x: 4, y: 4, z: 8, core: 2. Of those that a mesh axis runs over, the one named last changes fastest.
Arguments:
- queries: bfloat16 [8192, 8192], P('ctx', 'head'), may hold values from -20 to 20
- keys: bfloat16 [8192, 1024], P('ctx', 'head'), may hold values from -4 to 4
- values: bfloat16 [8192, 1024], P('ctx', 'head'), may hold values from -6 to 6
- grad_out: bfloat16 [8192, 8192], P('ctx', 'head'), may hold values from -6 to 6
- key_blocks: int32 [64, 6], replicated, may hold values from 0 to 63, as said below
- key_count: int32 [64], replicated, may hold values from 2 to 6
Outputs:
- attended: bfloat16 [8192, 8192], P('ctx', 'head')
- grad_q: bfloat16 [8192, 8192], P('ctx', 'head')
- grad_k: bfloat16 [8192, 1024], P('ctx', 'head')
- grad_v: bfloat16 [8192, 1024], P('ctx', 'head')
Inputs may be any that keep to these rules, and one draw needn't show every extreme that they name: `key_blocks`: the listed key blocks of block b lie outside the range of 2 blocks that holds b (ranges begin at multiples of 2), each in a different range. Over the used slots of all query blocks of one range, at most 1 name blocks of any one other range; in every draw the query blocks of one range use all their 6 slots, so that this most and 12 used slots of one range are reached.
All inputs are finite; a program needn't handle non-finite values.
Results may differ from a plain program's by a relative error of at most 0.034.
Values may be sent and summed in bfloat16 or wider, within the bound.
A program may use at most 64 MiB of HBM per device.

v0:
```python
import math

import jax
import jax.numpy as jnp
from jax import lax
from jax.sharding import PartitionSpec as P

QH = 64
KVH = 8
DH = 128
BLOCK = 128
KSLOTS = 6


def attend(q_blk, o_blk, near_k, near_v, column, scaling):
    scores = (
        jnp.einsum("qhgd,khd->hgqk", q_blk, near_k, preferred_element_type=jnp.float32) * scaling
    )
    scores = jnp.where(column, scores, -1e30)
    row_max = jnp.max(scores, axis=-1, keepdims=True)
    expo_terms = jnp.where(column, jnp.exp(scores - row_max), 0.0)
    prob_rows = expo_terms / jnp.sum(expo_terms, axis=-1, keepdims=True)
    weights = prob_rows.astype(jnp.bfloat16)
    attended = jnp.einsum(
        "hgqk,khd->qhgd", weights, near_v, preferred_element_type=jnp.float32
    ).astype(jnp.bfloat16)
    delta_rows = jnp.sum(o_blk.astype(jnp.float32) * attended.astype(jnp.float32), axis=-1)
    grad_p = jnp.einsum("qhgd,khd->hgqk", o_blk, near_v, preferred_element_type=jnp.float32)
    grad_s = (
        prob_rows * (grad_p - jnp.transpose(delta_rows, (1, 2, 0))[..., None]) * scaling
    ).astype(jnp.bfloat16)
    grad_q = jnp.einsum(
        "hgqk,khd->qhgd", grad_s, near_k, preferred_element_type=jnp.float32
    ).astype(jnp.bfloat16)
    part_k = jnp.einsum("hgqk,qhgd->khd", grad_s, q_blk, preferred_element_type=jnp.float32)
    part_v = jnp.einsum("hgqk,qhgd->khd", weights, o_blk, preferred_element_type=jnp.float32)
    return (attended, grad_q, part_k, part_v)


def local(queries, keys, values, grad_out, key_blocks, key_count):
    q_loc, o_loc, k_loc, v_loc = (queries, grad_out, keys, values)
    contexts = lax.axis_size("ctx")
    position = lax.axis_index("ctx")
    row_count = q_loc.shape[0]
    blk_dev = row_count // BLOCK
    heads_loc = k_loc.shape[1] // DH
    group_size = QH // KVH
    tile_size = BLOCK * heads_loc * DH
    entries = blk_dev * KSLOTS
    slots_peer = (entries + contexts - 2) // (contexts - 1)
    key_width = (KSLOTS + 1) * BLOCK
    scaling = 1.0 / math.sqrt(DH)
    owners = (key_blocks // blk_dev).reshape(contexts, entries)
    within = (key_blocks % blk_dev).reshape(contexts, entries)
    is_live = (jnp.arange(KSLOTS)[None, :] < key_count[:, None]).reshape(contexts, entries)
    entry_ids = jnp.arange(entries)
    earlier = (
        (owners[:, :, None] == owners[:, None, :])
        & is_live[:, None, :]
        & (entry_ids[None, :] < entry_ids[:, None])[None]
    )
    rank_of = jnp.sum(earlier.astype(jnp.int32), axis=2)
    mine_owner = owners[position]
    mine_rank = rank_of[position]
    mine_live = is_live[position]
    kv_tiles = jnp.concatenate(
        [k_loc.reshape(blk_dev, tile_size), v_loc.reshape(blk_dev, tile_size)], axis=1
    )
    serve = (
        (is_live & (owners == position))[:, :, None, None]
        & (rank_of[:, :, None, None] == jnp.arange(slots_peer)[None, None, :, None])
        & (within[:, :, None, None] == jnp.arange(blk_dev)[None, None, None, :])
    )
    picker = jnp.any(serve, axis=1).reshape(contexts * slots_peer, blk_dev)
    outgoing = jnp.dot(
        picker.astype(jnp.bfloat16), kv_tiles, preferred_element_type=jnp.float32
    ).astype(jnp.bfloat16)
    incoming = lax.all_to_all(outgoing, "ctx", split_axis=0, concat_axis=0, tiled=True)
    target = mine_owner * slots_peer + mine_rank
    taker = (target[:, None] == jnp.arange(contexts * slots_peer)[None, :]) & mine_live[:, None]
    fetched = jnp.dot(
        taker.astype(jnp.bfloat16), incoming, preferred_element_type=jnp.float32
    ).astype(jnp.bfloat16)
    key_own = k_loc.reshape(blk_dev, 1, BLOCK, heads_loc, DH)
    value_own = v_loc.reshape(blk_dev, 1, BLOCK, heads_loc, DH)
    near_k = jnp.concatenate(
        [key_own, fetched[:, :tile_size].reshape(blk_dev, KSLOTS, BLOCK, heads_loc, DH)], axis=1
    ).reshape(blk_dev, key_width, heads_loc, DH)
    near_v = jnp.concatenate(
        [value_own, fetched[:, tile_size:].reshape(blk_dev, KSLOTS, BLOCK, heads_loc, DH)], axis=1
    ).reshape(blk_dev, key_width, heads_loc, DH)
    columns = jnp.repeat(
        jnp.concatenate(
            [jnp.ones((blk_dev, 1), dtype=bool), mine_live.reshape(blk_dev, KSLOTS)], axis=1
        ),
        BLOCK,
        axis=1,
    )
    q_tiles = q_loc.reshape(blk_dev, BLOCK, heads_loc, group_size, DH)
    o_tiles = o_loc.reshape(blk_dev, BLOCK, heads_loc, group_size, DH)

    def per_block(members):
        return attend(members[0], members[1], members[2], members[3], members[4], scaling)

    attended, grad_q, part_k, part_v = lax.map(
        per_block, (q_tiles, o_tiles, near_k, near_v, columns)
    )
    part_k = part_k.reshape(blk_dev, KSLOTS + 1, tile_size)
    part_v = part_v.reshape(blk_dev, KSLOTS + 1, tile_size)
    own_sums = jnp.concatenate([part_k[:, 0], part_v[:, 0]], axis=1)
    sent_terms = jnp.concatenate(
        [part_k[:, 1:].reshape(entries, tile_size), part_v[:, 1:].reshape(entries, tile_size)],
        axis=1,
    )
    outgoing_sums = jnp.dot(
        taker.astype(jnp.float32).T, sent_terms, precision=lax.Precision.HIGHEST
    )
    returned = lax.all_to_all(outgoing_sums, "ctx", split_axis=0, concat_axis=0, tiled=True)
    remote_sums = jnp.dot(picker.astype(jnp.float32).T, returned, precision=lax.Precision.HIGHEST)
    totals = own_sums + remote_sums
    grad_k = totals[:, :tile_size].astype(jnp.bfloat16).reshape(row_count, heads_loc * DH)
    grad_v = totals[:, tile_size:].astype(jnp.bfloat16).reshape(row_count, heads_loc * DH)
    attended = attended.reshape(row_count, heads_loc * group_size * DH)
    grad_q = grad_q.reshape(row_count, heads_loc * group_size * DH)
    return (attended, grad_q, grad_k, grad_v)


def solution(mesh):
    in_specs = (P("ctx", "head"), P("ctx", "head"), P("ctx", "head"), P("ctx", "head"), P(), P())
    out_specs = (P("ctx", "head"), P("ctx", "head"), P("ctx", "head"), P("ctx", "head"))
    return jax.shard_map(local, mesh=mesh, in_specs=in_specs, out_specs=out_specs, check_vma=False)
```

profile of v0, /device:TPU:8, one launch (start us, length us, event | category | flops | bytes accessed | tf_op | source)
XLA Modules:
  0.0 259.0 jit_solution(7295496209452770861)
XLA Ops:
  6.1 2.9 %reduce.11 = bf16[32,32768]{1,0:T(8,128)(2,1)} reduce(bf16[32,1,32768]{2,0,1:T(8,128)(2,1)S(1)} %fusion.36, bf16[]{:T(256)} %broadcast.106), dimensions={1}, to_apply=%copy.143.reduce_sub_computation | reduce | bytes 4194306 | tf_op jit(solution)/shard_map/all_to_all | solution.py:78
  9.0 4.6 %reshape.270 = bf16[32,2,16384]{2,1,0:T(2,128)(2,1)} reshape(bf16[32,32768]{1,0:T(8,128)(2,1)} %reduce.11) | data formatting | bytes 4194304
  13.6 11.5 %all-to-all-start = ((bf16[32,2,16384]{2,1,0:T(2,128)(2,1)}), bf16[32,2,16384]{2,1,0:T(2,128)(2,1)S(1)}, u32[]{:S(2)}, u32[]{:S(2)}) async-start(bf16[32,2,16384]{2,1,0:T(2,128)(2,1)} %reshape.270), calls=%async_computation | async-start | bytes 4194304 | tf_op jit(solution)/shard_map/all_to_all | solution.py:78
  27.8 47.3 %all-to-all-done = bf16[32,2,16384]{2,1,0:T(2,128)(2,1)S(1)} async-done(((bf16[32,2,16384]{2,1,0:T(2,128)(2,1)}), bf16[32,2,16384]{2,1,0:T(2,128)(2,1)S(1)}, u32[]{:S(2)}, u32[]{:S(2)}) %all-to-all-start) | async-done | bytes 2097184 | tf_op jit(solution)/shard_map/all_to_all | solution.py:78
  75.1 6.8 %reshape.271 = bf16[32,1,32768]{2,1,0:T(2,128)(2,1)} reshape(bf16[32,2,16384]{2,1,0:T(2,128)(2,1)S(1)} %all-to-all-done) | data formatting | bytes 4194304
  81.9 4.5 %convolution_convert_fusion.2 = bf16[12,32768]{1,0:T(8,128)(2,1)S(1)} fusion(bf16[32,1,32768]{2,1,0:T(2,128)(2,1)} %reshape.271, s32[12]{0:T(128)S(1)} %add_reduce_fusion, pred[12]{0:T(512)(128)(4,1)S(1)} %dynamic-slice_reduce_fusion.1), kind=kOutput, calls=%fused_computation.49 | convolution fusion | flops 25559808 | bytes 2883644 | tf_op jit(solution)/shard_map/dot_general | solution.py:81
  88.1 44.6 %while.16 = (s32[]{:T(128)}, bf16[2,128,1,8,128]{4,3,1,0,2:T(8,128)(2,1)}, bf16[2,128,1,8,128]{4,3,1,0,2:T(8,128)(2,1)}, f32[2,896,1,128]{3,1,0,2:T(8,128)}, f32...) while((s32[]{:T(128)}, ...), condition=%wide.region_6.7_spmd, body=%wide.region_2.6_spmd.sunk | while | flops 1431172096 | bytes 78165320 | solution.py:105
  91.3 2.1 convert_bitcast_fusion.2
  95.2 4.0 %fusion.93 = bf16[1,8,128,896]{2,3,1,0:T(8,128)(2,1)S(1)} fusion(f32[8,128]{1,0:T(8,128)S(1)} %bitcast.264, f32[8,128]{1,0:T(8,128)S(1)} %fusion.90, f32[8,128]{1,0:T(8,128)S(1)} %get-tuple-element.221, f32[896,128,8]{1,0,2:T(8,128)} %copy-done, pred[896]{0:T(1024)(128)(4,1)S(1)} %dynamic-slice_reduce_fusion.3, bf16[128,8,128]{2,1,0:T(8,128)(2,1)S(1)} %fusion.92, ...), kind=kOutput, calls=%fused_computation.3.clone.1 | convolution fusion | flops 243138560 | bytes 6011392 | tf_op jit(solution)/shard_map/while/body/eval_jaxpr/qhgd,khd->hgqk/dot_general | solution.py:28
  101.3 2.9 %copy.225 = bf16[8,128,896]{2,0,1:T(8,128)(2,1)} copy(bf16[8,128,896]{1,2,0:T(8,128)(2,1)S(1)} %convert_bitcast_fusion.2) | data formatting | bytes 3670016 | tf_op jit(solution)/shard_map/reshape.6
  104.3 2.1 convolution_bitcast_fusion.3
  107.6 1.5 fusion.94
  113.6 2.1 convert_bitcast_fusion.2
  117.4 4.0 %fusion.93 = bf16[1,8,128,896]{2,3,1,0:T(8,128)(2,1)S(1)} fusion(f32[8,128]{1,0:T(8,128)S(1)} %bitcast.264, f32[8,128]{1,0:T(8,128)S(1)} %fusion.90, f32[8,128]{1,0:T(8,128)S(1)} %get-tuple-element.221, f32[896,128,8]{1,0,2:T(8,128)} %copy-done, pred[896]{0:T(1024)(128)(4,1)S(1)} %dynamic-slice_reduce_fusion.3, bf16[128,8,128]{2,1,0:T(8,128)(2,1)S(1)} %fusion.92, ...), kind=kOutput, calls=%fused_computation.3.clone.1 | convolution fusion | flops 243138560 | bytes 6011392 | tf_op jit(solution)/shard_map/while/body/eval_jaxpr/qhgd,khd->hgqk/dot_general | solution.py:28
  123.6 2.9 %copy.225 = bf16[8,128,896]{2,0,1:T(8,128)(2,1)} copy(bf16[8,128,896]{1,2,0:T(8,128)(2,1)S(1)} %convert_bitcast_fusion.2) | data formatting | bytes 3670016 | tf_op jit(solution)/shard_map/reshape.6
  126.5 2.1 convolution_bitcast_fusion.3
  136.7 2.3 reshape.255
  140.1 2.4 reshape.256
  142.5 3.5 %convolution_bitcast_fusion.1 = f32[32,1,32768]{2,0,1:T(8,128)S(1)} fusion(f32[12,16384]{1,0:T(8,128)} %reshape.256, f32[12,16384]{1,0:T(8,128)} %reshape.255, s32[12]{0:T(128)S(1)} %add_reduce_fusion, pred[12]{0:T(512)(128)(4,1)S(1)} %dynamic-slice_reduce_fusion.1), kind=kOutput, calls=%fused_computation.46 | convolution fusion | flops 151388928 | bytes 5767228 | tf_op jit(solution)/shard_map/dot_general | solution.py:115
  146.0 6.3 %copy.154 = f32[32,1,32768]{2,1,0:T(1,128)} copy(f32[32,1,32768]{2,0,1:T(8,128)S(1)} %convolution_bitcast_fusion.1) | data formatting | bytes 8388608 | tf_op jit(solution)/shard_map/all_to_all | solution.py:118
  152.3 6.3 %all-to-all-start.1 = ((f32[32,1,32768]{2,1,0:T(1,128)}), f32[32,1,32768]{2,1,0:T(1,128)}, u32[]{:S(2)}, u32[]{:S(2)}) async-start(f32[32,1,32768]{2,1,0:T(1,128)} %copy.154), calls=%async_computation.1 | async-start | bytes 8388608 | tf_op jit(solution)/shard_map/all_to_all | solution.py:118
  158.8 2.4 copy_bitcast_fusion.3
  161.4 90.3 %all-to-all-done.1 = f32[32,1,32768]{2,1,0:T(1,128)} async-done(((f32[32,1,32768]{2,1,0:T(1,128)}), f32[32,1,32768]{2,1,0:T(1,128)}, u32[]{:S(2)}, u32[]{:S(2)}) %all-to-all-start.1) | async-done | bytes 4194336 | tf_op jit(solution)/shard_map/all_to_all | solution.py:118
  251.7 5.8 %fusion.37 = bf16[2,32768]{1,0:T(2,128)(2,1)S(1)} fusion(pred[32,2]{0,1:T(4,128)(4,1)S(1)} %fusion.49, f32[32,1,32768]{2,1,0:T(1,128)} %all-to-all-done.1, f32[2,16384]{1,0:T(2,128)S(1)} %get-tuple-element.147, f32[2,16384]{1,0:T(2,128)S(1)} %get-tuple-element.148), kind=kOutput, calls=%fused_computation.51 | convolution fusion | flops 25362432 | bytes 4587584 | tf_op jit(solution)/shard_map/dot_general | solution.py:119
  (116 shorter events, 37.2 us)
Async XLA Ops:
  9.0 16.5 %copy-start.7 = (bf16[256,1024]{1,0:T(8,128)(2,1)S(1)}, bf16[256,1024]{1,0:T(8,128)(2,1)}, u32[]{:S(2)}) copy-start(bf16[256,1024]{1,0:T(8,128)(2,1)} %param.8) | copy-start | bytes 1572868
  13.6 61.5 %all-to-all-start = ((bf16[32,2,16384]{2,1,0:T(2,128)(2,1)}), bf16[32,2,16384]{2,1,0:T(2,128)(2,1)S(1)}, u32[]{:S(2)}, u32[]{:S(2)}) async-start(bf16[32,2,16384]{2,1,0:T(2,128)(2,1)} %reshape.270), calls=%async_computation | async-start | bytes 4194304 | tf_op jit(solution)/shard_map/all_to_all | solution.py:78
  86.4 0.8 copy-start.8
  86.4 1.7 copy-start.9
  88.1 5.3 %copy-start.5 = (bf16[2,896,1,128]{3,1,2,0:T(8,128)(2,1)}, bf16[2,896,1,128]{3,1,2,0:T(8,128)(2,1)S(1)}, u32[]{:S(2)}) copy-start(bf16[2,896,1,128]{3,1,2,0:T(8,128)(2,1)S(1)} %get-tuple-element.257) | copy-start | bytes 1376260 | tf_op jit(solution)/shard_map/while
  88.1 7.0 %copy-start.3 = (bf16[2,128,1,8,128]{4,3,1,0,2:T(8,128)(2,1)}, bf16[2,128,1,8,128]{4,3,1,0,2:T(8,128)(2,1)S(1)}, u32[]{:S(2)}) copy-start(bf16[2,128,1,8,128]{4,3,1,0,2:T(8,128)(2,1)S(1)} %get-tuple-element.259) | copy-start | bytes 1572868 | tf_op jit(solution)/shard_map/while
  90.0 3.4 %copy-start = (f32[896,128,8]{1,0,2:T(8,128)}, f32[896,128,8]{1,0,2:T(8,128)S(1)}, u32[]{:S(2)}) copy-start(f32[896,128,8]{1,0,2:T(8,128)S(1)} %get-tuple-element.220) | copy-start | bytes 11010052 | tf_op jit(solution)/shard_map/while
  99.1 1.3 copy-start.1
  104.3 3.3 %copy-start.2 = (bf16[1,8,128,896]{2,3,1,0:T(8,128)(2,1)S(1)}, bf16[1,8,128,896]{2,3,1,0:T(8,128)(2,1)}, u32[]{:S(2)}) copy-start(bf16[1,8,128,896]{2,3,1,0:T(8,128)(2,1)} %copy-done.1) | copy-start | bytes 5505028 | tf_op jit(solution)/shard_map/while
  107.6 2.8 %copy-start.4 = (bf16[2,128,1,8,128]{4,3,1,0,2:T(8,128)(2,1)S(1)}, bf16[2,128,1,8,128]{4,3,1,0,2:T(8,128)(2,1)}, u32[]{:S(2)}) copy-start(bf16[2,128,1,8,128]{4,3,1,0,2:T(8,128)(2,1)} %copy-done.3) | copy-start | bytes 1572868 | tf_op jit(solution)/shard_map/while
  107.6 2.8 %copy-start.6 = (bf16[2,896,1,128]{3,1,2,0:T(8,128)(2,1)S(1)}, bf16[2,896,1,128]{3,1,2,0:T(8,128)(2,1)}, u32[]{:S(2)}) copy-start(bf16[2,896,1,128]{3,1,2,0:T(8,128)(2,1)} %copy-done.5) | copy-start | bytes 1376260 | tf_op jit(solution)/shard_map/while
  110.4 5.3 %copy-start.5 = (bf16[2,896,1,128]{3,1,2,0:T(8,128)(2,1)}, bf16[2,896,1,128]{3,1,2,0:T(8,128)(2,1)S(1)}, u32[]{:S(2)}) copy-start(bf16[2,896,1,128]{3,1,2,0:T(8,128)(2,1)S(1)} %get-tuple-element.257) | copy-start | bytes 1376260 | tf_op jit(solution)/shard_map/while
  110.4 7.0 %copy-start.3 = (bf16[2,128,1,8,128]{4,3,1,0,2:T(8,128)(2,1)}, bf16[2,128,1,8,128]{4,3,1,0,2:T(8,128)(2,1)S(1)}, u32[]{:S(2)}) copy-start(bf16[2,128,1,8,128]{4,3,1,0,2:T(8,128)(2,1)S(1)} %get-tuple-element.259) | copy-start | bytes 1572868 | tf_op jit(solution)/shard_map/while
  112.3 3.4 %copy-start = (f32[896,128,8]{1,0,2:T(8,128)}, f32[896,128,8]{1,0,2:T(8,128)S(1)}, u32[]{:S(2)}) copy-start(f32[896,128,8]{1,0,2:T(8,128)S(1)} %get-tuple-element.220) | copy-start | bytes 11010052 | tf_op jit(solution)/shard_map/while
  121.4 1.3 copy-start.1
  126.5 3.4 %copy-start.2 = (bf16[1,8,128,896]{2,3,1,0:T(8,128)(2,1)S(1)}, bf16[1,8,128,896]{2,3,1,0:T(8,128)(2,1)}, u32[]{:S(2)}) copy-start(bf16[1,8,128,896]{2,3,1,0:T(8,128)(2,1)} %copy-done.1) | copy-start | bytes 5505028 | tf_op jit(solution)/shard_map/while
  129.9 2.8 %copy-start.4 = (bf16[2,128,1,8,128]{4,3,1,0,2:T(8,128)(2,1)S(1)}, bf16[2,128,1,8,128]{4,3,1,0,2:T(8,128)(2,1)}, u32[]{:S(2)}) copy-start(bf16[2,128,1,8,128]{4,3,1,0,2:T(8,128)(2,1)} %copy-done.3) | copy-start | bytes 1572868 | tf_op jit(solution)/shard_map/while
  129.9 2.8 %copy-start.6 = (bf16[2,896,1,128]{3,1,2,0:T(8,128)(2,1)S(1)}, bf16[2,896,1,128]{3,1,2,0:T(8,128)(2,1)}, u32[]{:S(2)}) copy-start(bf16[2,896,1,128]{3,1,2,0:T(8,128)(2,1)} %copy-done.5) | copy-start | bytes 1376260 | tf_op jit(solution)/shard_map/while
  152.3 99.4 %all-to-all-start.1 = ((f32[32,1,32768]{2,1,0:T(1,128)}), f32[32,1,32768]{2,1,0:T(1,128)}, u32[]{:S(2)}, u32[]{:S(2)}) async-start(f32[32,1,32768]{2,1,0:T(1,128)} %copy.154), calls=%async_computation.1 | async-start | bytes 8388608 | tf_op jit(solution)/shard_map/all_to_all | solution.py:118
where the time goes:
time: 261 us; the launch traced here: 259 us
  waiting for transfers between devices  138 us (53%)
  local copies, waits for them, and re-layouts  55.3 us (21%)
  matrix products  35.4 us (14%)
  starting transfers between devices  17.8 us (7%)
  other arithmetic  11.7 us (4%)
    all_to_all x1, waiting for transfers between devices, local(): lax.all_to_all(outgoing_sums, 'ctx', split_axis=0, concat_axis=0, tiled=T...  90.3 us
    all_to_all x1, waiting for transfers between devices, local(): lax.all_to_all(outgoing, 'ctx', split_axis=0, concat_axis=0, tiled=True)  47.3 us
    unnamed x16, local copies, waits for them, and re-layouts  14.2 us
    all_to_all x1, starting transfers between devices, local(): lax.all_to_all(outgoing, 'ctx', split_axis=0, concat_axis=0, tiled=True)  11.5 us
    dot_general x2, matrix products, attend(): jnp.einsum('qhgd,khd->hgqk', o_blk, near_v, preferred_element_type=jnp.fl...  7.94 us
    all_to_all x1, starting transfers between devices, local(): lax.all_to_all(outgoing_sums, 'ctx', split_axis=0, concat_axis=0, tiled=T...  6.33 us
    all_to_all x1, local copies, waits for them, and re-layouts, local(): lax.all_to_all(outgoing_sums, 'ctx', split_axis=0, concat_axis=0, tiled=T...  6.28 us
    another operation x4, local copies, waits for them, and re-layouts  5.94 us
  transfers between devices with their start and end apart: 2, of which 2 were waited for; matrix products, arithmetic and copies ran while one was open for 2% of the time, Pallas kernels for 0%

commit v1 on v0

v1 whole, which is shorter than its diff:
```python
import functools, math
import jax, jax.numpy as jnp
from jax import lax
from jax.experimental import pallas as pl
from jax.experimental.pallas import tpu as pltpu
from jax.sharding import PartitionSpec as P

QH = 64
KVH = 8
DH = 128
BLOCK = 128
KSLOTS = 6
NSLOT = KSLOTS + 1
GROUP = QH // KVH
SCALING = 1.0 / math.sqrt(DH)
LOG2E = 1.4426950408889634
NEG = -1e30


def attn_kernel(kb, kc, pos, q_ref, o_ref, own_ref, *rest):
    far = rest[:KSLOTS]
    att_ref, gq_ref, gown_ref, contrib_ref = rest[KSLOTS:KSLOTS + 4]
    k_s, v_s, kt_s, vt_s, s_s, dp_s, p_s, ds_s, dk_s, dv_s = rest[KSLOTS + 4:]
    b = pl.program_id(0)
    blk = pos[0] * pl.num_programs(0) + b
    count = kc[blk]

    @pl.when(b == 0)
    def _():
        contrib_ref[...] = jnp.zeros_like(contrib_ref)

    for s in range(NSLOT):
        src = own_ref if s == 0 else far[s - 1]
        rows = slice(s * BLOCK, (s + 1) * BLOCK)
        k = src[:, :DH]
        v = src[:, DH:]
        k_s[rows, :] = k
        v_s[rows, :] = v
        kt_s[:, rows] = k.T
        vt_s[:, rows] = v.T
    bias = [None] + [jnp.where(s < count, 0.0, NEG).astype(jnp.float32) for s in range(KSLOTS)]
    c = SCALING * LOG2E
    nt = (((1,), (1,)), ((), ()))

    for pair in range(GROUP // 2):
        cols = [slice((2 * pair + i) * DH, (2 * pair + i + 1) * DH) for i in range(2)]
        q2 = jnp.concatenate([q_ref[:, cols[0]], q_ref[:, cols[1]]], axis=0)
        o2 = jnp.concatenate([o_ref[:, cols[0]], o_ref[:, cols[1]]], axis=0)
        m = None
        for s in range(NSLOT):
            rows = slice(s * BLOCK, (s + 1) * BLOCK)
            sc = lax.dot_general(k_s[rows, :], q2, nt, preferred_element_type=jnp.float32)
            s_s[rows, :] = sc
            top = jnp.max(sc, axis=0, keepdims=True)
            if s > 0:
                top = top + bias[s]
            m = top if m is None else jnp.maximum(m, top)
        mc = m * c
        total = None
        for s in range(NSLOT):
            rows = slice(s * BLOCK, (s + 1) * BLOCK)
            off = -mc if s == 0 else bias[s] - mc
            e = jnp.exp2(s_s[rows, :] * c + off)
            s_s[rows, :] = e
            part = jnp.sum(e, axis=0, keepdims=True)
            total = part if total is None else total + part
        inv = 1.0 / total
        for s in range(NSLOT):
            rows = slice(s * BLOCK, (s + 1) * BLOCK)
            p_s[rows, :] = (s_s[rows, :] * inv).astype(jnp.bfloat16)
        p16 = p_s[...]
        out_t = jnp.dot(vt_s[...], p16, preferred_element_type=jnp.float32)
        att_t = out_t.astype(jnp.bfloat16)
        o_t = o2.T.astype(jnp.float32)
        delta = jnp.sum(o_t * att_t.astype(jnp.float32), axis=0, keepdims=True)
        att = att_t.T
        att_ref[:, cols[0]] = att[:BLOCK]
        att_ref[:, cols[1]] = att[BLOCK:]
        dv = jnp.dot(p16, o2, preferred_element_type=jnp.float32)
        if pair == 0:
            dv_s[...] = dv
        else:
            dv_s[...] += dv
        inv_c = inv * SCALING
        for s in range(NSLOT):
            rows = slice(s * BLOCK, (s + 1) * BLOCK)
            dp = lax.dot_general(v_s[rows, :], o2, nt, preferred_element_type=jnp.float32)
            ds_s[rows, :] = ((s_s[rows, :] * inv_c) * (dp - delta)).astype(jnp.bfloat16)
        ds16 = ds_s[...]
        gq = jnp.dot(kt_s[...], ds16, preferred_element_type=jnp.float32).astype(jnp.bfloat16).T
        gq_ref[:, cols[0]] = gq[:BLOCK]
        gq_ref[:, cols[1]] = gq[BLOCK:]
        dk = jnp.dot(ds16, q2, preferred_element_type=jnp.float32)
        if pair == 0:
            dk_s[...] = dk
        else:
            dk_s[...] += dk
    gown_ref[:, :DH] = dk_s[:BLOCK, :]
    gown_ref[:, DH:] = dv_s[:BLOCK, :]
    for s in range(KSLOTS):
        rows = slice((s + 1) * BLOCK, (s + 2) * BLOCK)

        @pl.when(s < count)
        def _():
            at = kb[blk * KSLOTS + s]
            contrib_ref[at, :, :DH] = dk_s[rows, :].astype(jnp.bfloat16)
            contrib_ref[at, :, DH:] = dv_s[rows, :].astype(jnp.bfloat16)


def attention(kb, kc, pos, q, o, own, every):
    rows, width = q.shape
    blocks = rows // BLOCK
    n_all = every.shape[0]
    row = lambda b, kb, kc, pos: (b, 0)
    def far(s):
        return pl.BlockSpec((pl.Squeezed(), BLOCK, 2 * DH), lambda b, kb, kc, pos: (kb[(pos[0] * blocks + b) * KSLOTS + s], 0, 0))
    wide = NSLOT * BLOCK
    spec = pltpu.PrefetchScalarGridSpec(
        num_scalar_prefetch=3,
        grid=(blocks,),
        in_specs=[pl.BlockSpec((BLOCK, width), row), pl.BlockSpec((BLOCK, width), row), pl.BlockSpec((BLOCK, 2 * DH), row)] + [far(s) for s in range(KSLOTS)],
        out_specs=[pl.BlockSpec((BLOCK, width), row), pl.BlockSpec((BLOCK, width), row), pl.BlockSpec((BLOCK, 2 * DH), row), pl.BlockSpec((n_all, BLOCK, 2 * DH), lambda b, kb, kc, pos: (0, 0, 0))],
        scratch_shapes=[pltpu.VMEM((wide, DH), jnp.bfloat16)] * 2 + [pltpu.VMEM((DH, wide), jnp.bfloat16)] * 2
        + [pltpu.VMEM((wide, 2 * BLOCK), jnp.float32)] * 2 + [pltpu.VMEM((wide, 2 * BLOCK), jnp.bfloat16)] * 2 + [pltpu.VMEM((wide, DH), jnp.float32)] * 2,
    )
    return pl.pallas_call(
        attn_kernel,
        grid_spec=spec,
        out_shape=[jax.ShapeDtypeStruct((rows, width), jnp.bfloat16)] * 2 + [jax.ShapeDtypeStruct((rows, 2 * DH), jnp.float32), jax.ShapeDtypeStruct((n_all, BLOCK, 2 * DH), jnp.bfloat16)],
        compiler_params=pltpu.CompilerParams(vmem_limit_bytes=48 << 20),
        name="attention",
    )(kb, kc, pos, q, o, own, *([every] * KSLOTS))


def local(queries, keys, values, grad_out, key_blocks, key_count):
    rows = queries.shape[0]
    pos = lax.axis_index("ctx").astype(jnp.int32).reshape(1)
    own = jnp.concatenate([keys, values], axis=1)
    every = lax.all_gather(own, "ctx", axis=0, tiled=True).reshape(-1, BLOCK, 2 * DH)
    att, gq, gown, contrib = attention(key_blocks.reshape(-1), key_count, pos, queries, grad_out, own, every)
    mine = lax.psum_scatter(contrib, "ctx", scatter_dimension=0, tiled=True)
    total = (gown + mine.reshape(rows, 2 * DH).astype(jnp.float32)).astype(jnp.bfloat16)
    return att, gq, total[:, :DH], total[:, DH:]


def solution(mesh):
    in_specs = (P("ctx", "head"), P("ctx", "head"), P("ctx", "head"), P("ctx", "head"), P(), P())
    out_specs = (P("ctx", "head"), P("ctx", "head"), P("ctx", "head"), P("ctx", "head"))
    return jax.shard_map(local, mesh=mesh, in_specs=in_specs, out_specs=out_specs, check_vma=False)
```

time: 261 us -> 341 us (1.31)
  waiting for transfers between devices: 138 us -> 304 us
  local copies, waits for them, and re-layouts: 55.3 us -> 9.53 us
  matrix products: 35.4 us -> 0 us
  starting transfers between devices: 17.8 us -> 0.08 us
  between operations: 0.86 us -> 14.1 us
  Pallas kernels: 0 us -> 11.6 us
  other arithmetic: 11.7 us -> 0.93 us
    reduce_scatter x0 -> x1, waiting for transfers between devices: none -> 219 us  [local(): mine = lax.psum_scatter(contrib, 'ctx', scatter_dimension=0, tiled=True)]
    all_to_all x2 -> x0, waiting for transfers between devices: 138 us -> none  [the longest x1 90.3 us: local(): lax.all_to_all(outgoing_sums, 'ctx', split_axis=0, concat_axis=0, tiled=T...]
    all_gather x0 -> x1, waiting for transfers between devices: none -> 85.3 us  [local(): lax.all_gather(own, 'ctx', axis=0, tiled=True).reshape(-1, BLOCK, 2 * DH)]
    dot_general x16 -> x0, matrix products: 35.4 us -> none  [the longest x2 7.94 us: attend(): jnp.einsum('qhgd,khd->hgqk', o_blk, near_v, preferred_element_type=jnp.fl...]
    all_to_all x2 -> x0, starting transfers between devices: 17.8 us -> none  [the longest x1 11.5 us: local(): lax.all_to_all(outgoing, 'ctx', split_axis=0, concat_axis=0, tiled=True)]
    reshape x11 -> x1, local copies, waits for them, and re-layouts: 13.2 us -> 0.14 us  [local(): key_blocks.reshape(-1)]
    pallas_call x0 -> x1, Pallas kernels: none -> 11.6 us  [attention(): pl.pallas_call(attn_kernel, grid_spec=spec, out_shape=[jax.ShapeDtypeStru...]
    all_to_all x2 -> x0, local copies, waits for them, and re-layouts: 6.8 us -> none  [the longest x1 6.28 us: local(): lax.all_to_all(outgoing_sums, 'ctx', split_axis=0, concat_axis=0, tiled=T...]
  transfers between devices with their start and end apart: 2 -> 2, of which waited for: 2 -> 2; matrix products, arithmetic and copies ran while one was open for 2% -> 0% of each run, Pallas kernels for 0% -> 0%
where the time goes in v1:
time: 341 us; the launch traced here: 340 us
  waiting for transfers between devices  304 us (89%)
  between operations  14.1 us (4%)
  Pallas kernels  11.6 us (3%)
  local copies, waits for them, and re-layouts  9.53 us (3%)
    reduce_scatter x1, waiting for transfers between devices, local(): mine = lax.psum_scatter(contrib, 'ctx', scatter_dimension=0, tiled=True)  219 us
    all_gather x1, waiting for transfers between devices, local(): lax.all_gather(own, 'ctx', axis=0, tiled=True).reshape(-1, BLOCK, 2 * DH)  85.3 us
    pallas_call x1, Pallas kernels, attention(): pl.pallas_call(attn_kernel, grid_spec=spec, out_shape=[jax.ShapeDtypeStru...  11.6 us
    unnamed x14, local copies, waits for them, and re-layouts  7.88 us
  transfers between devices with their start and end apart: 2, of which 2 were waited for; matrix products, arithmetic and copies ran while one was open for 0% of the time, Pallas kernels for 0%

profile of v1, /device:TPU:8, one launch (start us, length us, event | category | flops | bytes accessed | tf_op | source)
XLA Modules:
  0.0 340.3 jit_solution(6088162099292799234)
XLA Ops:
  7.2 0.0 all-gather.2.cloned.1.call-start
  7.2 0.9 constant_dynamic-update-slice_fusion.1
  8.1 0.9 constant_dynamic-update-slice_fusion.own_ref
  8.9 0.0 copy-start.1
  8.9 0.6 copy-done.1
  9.6 0.0 all-gather.2.cloned.1.call-update
  9.6 0.0 reduce-scatter.2.cloned.1.call-start
  9.7 0.8 copy.10
  10.4 0.1 reshape.20.kb
  10.6 85.3 %all-gather.2.cloned.1.call-done = bf16[8192,256]{1,0:T(8,128)(2,1)} async-done(((bf16[256,256]{1,0:T(8,128)(2,1)}), bf16[8192,256]{1,0:T(8,128)(2,1)}) %all-gather.2.cloned.1.call-update) | async-done | bytes 4194320 | tf_op jit(solution)/shard_map/all_gather | solution.py:139
  95.8 0.0 copy-start.2
  95.8 0.9 copy-done.2
  96.7 0.0 copy-start.3
  96.7 1.0 copy-done.3
  97.8 0.0 copy-start.4
  97.8 1.0 copy-done.4
  98.8 0.0 copy-start.5
  98.8 0.7 copy-done.5
  99.5 11.6 %attention.1 = (bf16[256,1024]{1,0:T(8,128)(2,1)}, bf16[256,1024]{1,0:T(8,128)(2,1)}, f32[256,256]{1,0:T(8,128)S(1)}, bf16[64,128,256]{2,1,0:T(8,128)(2,1)S(1)}) custom-call(s32[384]{0:T(512)S(1)} %reshape.20.kb, s32[64]{0:T(128)S(1)} %copy-done.5, s32[1]{0:T(128)} %bitcast.pos, bf16[256,1024]{1,0:T(8,128)(2,1)S(1)} %copy-done.3, ...), custom_call_target="tpu_custom_call" | custom-call | tf_op jit(solution)/shard_map/attention/pallas_call | solution.py:126
  111.1 2.0 copy-done
  113.1 0.0 reduce-scatter.2.cloned.1.call-update
  113.1 218.7 %reduce-scatter.2.cloned.1.call-done = bf16[2,128,256]{2,1,0:T(8,128)(2,1)} async-done(((bf16[64,128,256]{2,1,0:T(8,128)(2,1)}), bf16[2,128,256]{2,1,0:T(8,128)(2,1)}) %reduce-scatter.2.cloned.1.call-update) | async-done | bytes 131088 | tf_op jit(solution)/shard_map/reduce_scatter | solution.py:141
  331.8 0.9 fusion
  332.8 0.7 fusion.1
  (1 shorter events, 0.0 us)
Async XLA Ops:
  7.2 88.7 %all-gather.2.cloned.1.call-start = ((), (), s32[]{:S(2)}) async-start(), calls=%async_computation.1 | async-start | bytes 4325376 | tf_op jit(solution)/shard_map/all_gather | solution.py:139
  8.9 0.7 copy-start.1
  9.6 322.2 %reduce-scatter.2.cloned.1.call-start = ((), (), s32[]{:S(2)}) async-start(), calls=%async_computation.2 | async-start | bytes 4325376 | tf_op jit(solution)/shard_map/reduce_scatter | solution.py:141
  95.8 0.9 copy-start.2
  96.7 1.0 copy-start.3
  97.8 1.0 copy-start.4
  98.8 0.7 copy-start.5
  111.1 2.0 copy-start
Sparse Core Ops, SparseCore 0:
  11.2 84.6 all-gather.1
  113.2 218.5 reduce-scatter.1

commit v2 on v1

--- a/solution.py
+++ b/solution.py
@@ -17,23 +17,23 @@
 NEG = -1e30
 
 
-def attn_kernel(kb, kc, pos, q_ref, o_ref, own_ref, *rest):
-    far = rest[:KSLOTS]
-    att_ref, gq_ref, gown_ref, contrib_ref = rest[KSLOTS:KSLOTS + 4]
-    k_s, v_s, kt_s, vt_s, s_s, dp_s, p_s, ds_s, dk_s, dv_s = rest[KSLOTS + 4:]
+def attn_kernel(kb, kc, pos, q_ref, o_ref, k_own, v_own, *rest):
+    far_k, far_v = rest[:KSLOTS], rest[KSLOTS:2 * KSLOTS]
+    att_ref, gq_ref, gk_ref, gv_ref, ck_ref, cv_ref = rest[2 * KSLOTS:2 * KSLOTS + 6]
+    k_s, v_s, kt_s, vt_s, s_s, p_s, ds_s, dk_s, dv_s = rest[2 * KSLOTS + 6:]
     b = pl.program_id(0)
     blk = pos[0] * pl.num_programs(0) + b
     count = kc[blk]
 
     @pl.when(b == 0)
     def _():
-        contrib_ref[...] = jnp.zeros_like(contrib_ref)
+        ck_ref[...] = jnp.zeros_like(ck_ref)
+        cv_ref[...] = jnp.zeros_like(cv_ref)
 
     for s in range(NSLOT):
-        src = own_ref if s == 0 else far[s - 1]
         rows = slice(s * BLOCK, (s + 1) * BLOCK)
-        k = src[:, :DH]
-        v = src[:, DH:]
+        k = (k_own if s == 0 else far_k[s - 1])[...]
+        v = (v_own if s == 0 else far_v[s - 1])[...]
         k_s[rows, :] = k
         v_s[rows, :] = v
         kt_s[:, rows] = k.T
@@ -95,52 +95,330 @@
             dk_s[...] = dk
         else:
             dk_s[...] += dk
-    gown_ref[:, :DH] = dk_s[:BLOCK, :]
-    gown_ref[:, DH:] = dv_s[:BLOCK, :]
+    gk_ref[...] = dk_s[:BLOCK, :]
+    gv_ref[...] = dv_s[:BLOCK, :]
     for s in range(KSLOTS):
         rows = slice((s + 1) * BLOCK, (s + 2) * BLOCK)
 
         @pl.when(s < count)
         def _():
             at = kb[blk * KSLOTS + s]
-            contrib_ref[at, :, :DH] = dk_s[rows, :].astype(jnp.bfloat16)
-            contrib_ref[at, :, DH:] = dv_s[rows, :].astype(jnp.bfloat16)
-
-
-def attention(kb, kc, pos, q, o, own, every):
+            ck_ref[at] = dk_s[rows, :].astype(jnp.bfloat16)
+            cv_ref[at] = dv_s[rows, :].astype(jnp.bfloat16)
+
+
+def attention(kb, kc, pos, q, o, k_own, v_own, k_all, v_all):
     rows, width = q.shape
     blocks = rows // BLOCK
-    n_all = every.shape[0]
+    n_all = k_all.shape[0]
     row = lambda b, kb, kc, pos: (b, 0)
+
     def far(s):
-        return pl.BlockSpec((pl.Squeezed(), BLOCK, 2 * DH), lambda b, kb, kc, pos: (kb[(pos[0] * blocks + b) * KSLOTS + s], 0, 0))
+        def index(b, kb, kc, pos):
+            blk = pos[0] * blocks + b
+            return (kb[blk * KSLOTS + jnp.where(s < kc[blk], s, 0)], 0, 0)
+
+        return pl.BlockSpec((pl.Squeezed(), BLOCK, DH), index)
+
+    wide_spec = pl.BlockSpec((BLOCK, width), row)
+    own_spec = pl.BlockSpec((BLOCK, DH), row)
+    all_spec = pl.BlockSpec((n_all, BLOCK, DH), lambda b, kb, kc, pos: (0, 0, 0))
     wide = NSLOT * BLOCK
     spec = pltpu.PrefetchScalarGridSpec(
         num_scalar_prefetch=3,
         grid=(blocks,),
-        in_specs=[pl.BlockSpec((BLOCK, width), row), pl.BlockSpec((BLOCK, width), row), pl.BlockSpec((BLOCK, 2 * DH), row)] + [far(s) for s in range(KSLOTS)],
-        out_specs=[pl.BlockSpec((BLOCK, width), row), pl.BlockSpec((BLOCK, width), row), pl.BlockSpec((BLOCK, 2 * DH), row), pl.BlockSpec((n_all, BLOCK, 2 * DH), lambda b, kb, kc, pos: (0, 0, 0))],
+        in_specs=[wide_spec] * 2 + [own_spec] * 2 + [far(s) for s in range(KSLOTS)] * 2,
+        out_specs=[wide_spec] * 2 + [own_spec] * 2 + [all_spec] * 2,
         scratch_shapes=[pltpu.VMEM((wide, DH), jnp.bfloat16)] * 2 + [pltpu.VMEM((DH, wide), jnp.bfloat16)] * 2
-        + [pltpu.VMEM((wide, 2 * BLOCK), jnp.float32)] * 2 + [pltpu.VMEM((wide, 2 * BLOCK), jnp.bfloat16)] * 2 + [pltpu.VMEM((wide, DH), jnp.float32)] * 2,
+        + [pltpu.VMEM((wide, 2 * BLOCK), jnp.float32)] + [pltpu.VMEM((wide, 2 * BLOCK), jnp.bfloat16)] * 2 + [pltpu.VMEM((wide, DH), jnp.float32)] * 2,
     )
+    out = lambda shape, dtype: jax.ShapeDtypeStruct(shape, dtype)
     return pl.pallas_call(
         attn_kernel,
         grid_spec=spec,
-        out_shape=[jax.ShapeDtypeStruct((rows, width), jnp.bfloat16)] * 2 + [jax.ShapeDtypeStruct((rows, 2 * DH), jnp.float32), jax.ShapeDtypeStruct((n_all, BLOCK, 2 * DH), jnp.bfloat16)],
+        out_shape=[out((rows, width), jnp.bfloat16)] * 2 + [out((rows, DH), jnp.float32)] * 2 + [out((n_all, BLOCK, DH), jnp.bfloat16)] * 2,
         compiler_params=pltpu.CompilerParams(vmem_limit_bytes=48 << 20),
         name="attention",
-    )(kb, kc, pos, q, o, own, *([every] * KSLOTS))
+    )(kb, kc, pos, q, o, k_own, v_own, *([k_all] * KSLOTS), *([v_all] * KSLOTS))
+
+
+XN = 4
+MESH = pl.DeviceIdType.MESH
+
+
+class Tree:
+    def __init__(self, first, n):
+        position = lax.axis_index("ctx")
+        sizes = {"x": XN, "z": n // XN}
+        coords = {"x": lax.rem(position, XN), "z": lax.div(position, XN)}
+        self.first = first
+        self.na, self.nb = sizes[first], sizes["z" if first == "x" else "x"]
+        self.a, self.b = coords[first], coords["z" if first == "x" else "x"]
+
+    def at(self, da, db):
+        a = lax.rem(self.a + (da % self.na), self.na)
+        b = lax.rem(self.b + (db % self.nb), self.nb)
+        return b * XN + a if self.first == "x" else a * XN + b
+
+    def keys(self):
+        out = [(1, 0, d, t) for t in range(1, self.na // 2 + 1) for d in (1, -1)]
+        for da in range(self.na):
+            out += [(2, da, d, t) for t in range(1, self.nb // 2 + 1) for d in (1, -1)]
+        return out
+
+    def length(self, stage):
+        return self.na if stage == 1 else self.nb
+
+    def step(self, stage, d):
+        return self.at(d, 0) if stage == 1 else self.at(0, d)
+
+    def span(self, stage, d, t, rows):
+        if t * 2 < self.length(stage):
+            return pl.ds(0, rows)
+        return pl.ds(0 if d == 1 else rows // 2, rows // 2)
+
+
+def far_first(n):
+    return sorted(range(n), key=lambda o: (-min(o, n - o), o))
+
+
+def meet(n):
+    barrier = pltpu.get_barrier_semaphore()
+    tree = Tree("x", n)
+    for stage in (1, 2):
+        for d in (1, -1):
+            pl.semaphore_signal(barrier, inc=1, device_id={"ctx": tree.step(stage, d)}, device_id_type=MESH)
+    pl.semaphore_wait(barrier, 4)
+
+
+def gather_kernel(n, k_ref, v_ref, k_all, v_all, send_sem, recv_sem):
+    rows = k_ref.shape[0]
+    trees = [Tree("x", n), Tree("z", n)]
+    own = [k_ref, v_ref]
+    every = [k_all, v_all]
+    number = {}
+    for i, tree in enumerate(trees):
+        for key in tree.keys():
+            number[(i,) + key] = len(number)
+    meet(n)
+    sent = []
+
+    def send(i, stage, da, d, t, src, slot):
+        tree = trees[i]
+        span = tree.span(stage, d, t, rows)
+        at = number[(i, stage, da, d, t)]
+        copy = pltpu.make_async_remote_copy(
+            src_ref=src.at[span], dst_ref=every[i].at[slot, span],
+            send_sem=send_sem.at[at], recv_sem=recv_sem.at[at],
+            device_id={"ctx": tree.step(stage, d)}, device_id_type=MESH)
+        copy.start()
+        sent.append(copy)
+
+    def origin(i, stage, da, d, t):
+        tree = trees[i]
+        return tree.at(-d * t, 0) if stage == 1 else tree.at(da, -d * t)
+
+    def await_one(i, stage, da, d, t):
+        tree = trees[i]
+        slot = origin(i, stage, da, d, t)
+        span = tree.span(stage, d, t, rows)
+        at = number[(i, stage, da, d, t)]
+        pltpu.make_async_remote_copy(
+            src_ref=every[i].at[slot, span], dst_ref=every[i].at[slot, span],
+            send_sem=send_sem.at[at], recv_sem=recv_sem.at[at],
+            device_id={"ctx": tree.step(stage, -d)}, device_id_type=MESH).wait_recv()
+        if t * 2 < tree.length(stage):
+            send(i, stage, da, d, t + 1, every[i].at[slot], slot)
+
+    def spread(i, da):
+        slot = trees[i].at(da, 0)
+        src = own[i] if da == 0 else every[i].at[slot]
+        for d in (1, -1):
+            send(i, 2, da, d, 1, src, slot)
+
+    for i in (1, 0):
+        for d in (1, -1):
+            send(i, 1, 0, d, 1, own[i], trees[i].at(0, 0))
+    for i in (0, 1):
+        spread(i, 0)
+
+    events = []
+    for i, tree in enumerate(trees):
+        pace = 1.2
+        for t in range(1, tree.na // 2 + 1):
+            events.append((1.0 + 1.3 * (t - 1), i, 1, 0, t))
+        near = [o for o in reversed(far_first(tree.na))]
+        for j, da in enumerate(near):
+            for t in range(1, tree.nb // 2 + 1):
+                events.append((1.5 + pace * j + pace * tree.na * (t - 1), i, 2, da, t))
+    for _, i, stage, da, t in sorted(events):
+        tree = trees[i]
+        for d in (1, -1):
+            await_one(i, stage, da, d, t)
+            if stage == 1 and t * 2 < tree.na:
+                spread(i, (-d * t) % tree.na)
+        if stage == 1 and t * 2 == tree.na:
+            spread(i, t)
+    for copy in sent:
+        copy.wait_send()
+
+
+def gather(n, k, v, copies):
+    shape = jax.ShapeDtypeStruct((n,) + k.shape, k.dtype)
+    return pl.pallas_call(
+        functools.partial(gather_kernel, n),
+        out_shape=[shape, shape],
+        in_specs=[pl.BlockSpec(memory_space=pl.ANY)] * 2,
+        out_specs=[pl.BlockSpec(memory_space=pl.ANY)] * 2,
+        scratch_shapes=[pltpu.SemaphoreType.DMA((copies,))] * 2,
+        compiler_params=pltpu.CompilerParams(collective_id=0, has_side_effects=True),
+        name="gather",
+    )(k, v)
+
+
+def scatter_kernel(n, ck_ref, cv_ref, gk_ref, gv_ref, outk_ref, outv_ref, land, sums_k, sums_v, send_sem, recv_sem):
+    rows = gk_ref.shape[0]
+    trees = [Tree("x", n), Tree("z", n)]
+    terms = [ck_ref, cv_ref]
+    sums = [sums_k, sums_v]
+    number = {}
+    for i, tree in enumerate(trees):
+        for key in tree.keys():
+            number[(i,) + key] = len(number)
+    meet(n)
+    sent = []
+
+    def send(i, stage, da, d, t, src):
+        tree = trees[i]
+        span = tree.span(stage, d, t, rows)
+        at = number[(i, stage, da, d, t)]
+        copy = pltpu.make_async_remote_copy(
+            src_ref=src.at[span], dst_ref=land.at[at, span],
+            send_sem=send_sem.at[at], recv_sem=recv_sem.at[at],
+            device_id={"ctx": tree.step(stage, -d)}, device_id_type=MESH)
+        copy.start()
+        sent.append(copy)
+
+    def arrive(i, stage, da, d, t):
+        tree = trees[i]
+        span = tree.span(stage, d, t, rows)
+        at = number[(i, stage, da, d, t)]
+        pltpu.make_async_remote_copy(
+            src_ref=land.at[at, span], dst_ref=land.at[at, span],
+            send_sem=send_sem.at[at], recv_sem=recv_sem.at[at],
+            device_id={"ctx": tree.step(stage, d)}, device_id_type=MESH).wait_recv()
+        return at, span
+
+    def pass_on(i, stage, da, d, t, load):
+        tree = trees[i]
+        at, span = arrive(i, stage, da, d, t + 1)
+        half = rows // 2
+        whole = (t + 1) * 2 < tree.length(stage)
+        for part in (0, 1):
+            here = pl.ds(part * half, half)
+            mine = load(here)
+            if whole or part == (0 if d == 1 else 1):
+                mine = (mine.astype(jnp.float32) + land[at, here].astype(jnp.float32)).astype(jnp.bfloat16)
+            land[at, here] = mine
+        send(i, stage, da, d, t, land.at[at])
+
+    def close(i, da):
+        tree = trees[i]
+        first, _ = arrive(i, 2, da, 1, 1)
+        second, _ = arrive(i, 2, da, -1, 1)
+        total = land[first].astype(jnp.float32) + land[second].astype(jnp.float32)
+        if da != 0:
+            total = total + terms[i][tree.at(da, 0)].astype(jnp.float32)
+            sums[i][da] = total.astype(jnp.bfloat16)
+            if da * 2 == tree.na:
+                for d in (1, -1):
+                    send(i, 1, 0, d, da, sums[i].at[da])
+            return
+        out = (outk_ref, outv_ref)[i]
+        grown = (gk_ref, gv_ref)[i]
+        for d in (1, -1):
+            at, _ = arrive(i, 1, 0, d, 1)
+            total = total + land[at].astype(jnp.float32)
+        out[...] = (total + grown[...]).astype(jnp.bfloat16)
+
+    def start(i, da):
+        tree = trees[i]
+        for d in (1, -1):
+            t = tree.nb // 2
+            send(i, 2, da, d, t, terms[i].at[tree.at(da, t)])
+
+    orders = [far_first(tree.na) for tree in trees]
+    for j in range(max(tree.na for tree in trees)):
+        for i in (0, 1):
+            if j < trees[i].na:
+                start(i, orders[i][j])
+    events = []
+    for i, tree in enumerate(trees):
+        top = tree.nb // 2
+        half = tree.na * 0.5
+        for j, da in enumerate(orders[i]):
+            for t in range(top - 1, 0, -1):
+                arrival = 0.5 * (j + 1) if t + 1 == top else half + tree.na * (top - t - 2) + j + 1
+                events.append((arrival, i, 2, da, t))
+            events.append((half + tree.na * (top - 2) + j + 1, i, 2, da, 0))
+        for t in range(tree.na // 2 - 1, 0, -1):
+            ready = half + tree.na * (top - 2) + 2 * (tree.na // 2 - t) + 2
+            events.append((ready, i, 1, 0, t))
+    events.sort()
+    for _, i, stage, da, t in events:
+        tree = trees[i]
+        if stage == 2 and t > 0:
+            for d in (1, -1):
+                target = tree.at(da, -d * t)
+                pass_on(i, 2, da, d, t, lambda here, i=i, target=target: terms[i][target, here])
+        elif stage == 2:
+            if da != 0:
+                close(i, da)
+        else:
+            for d in (1, -1):
+                pass_on(i, 1, 0, d, t, lambda here, i=i, o=(-d * t) % tree.na: sums[i][o, here])
+    for i in (0, 1):
+        close(i, 0)
+    for copy in sent:
+        copy.wait_send()
+
+
+def scatter(n, ck, cv, gk, gv, copies):
+    rows, width = gk.shape
+    vmem = pl.BlockSpec(memory_space=pltpu.VMEM)
+    shape = jax.ShapeDtypeStruct((rows, width), jnp.bfloat16)
+    return pl.pallas_call(
+        functools.partial(scatter_kernel, n),
+        out_shape=[shape, shape],
+        in_specs=[vmem] * 4,
+        out_specs=[vmem] * 2,
+        scratch_shapes=[pltpu.VMEM((copies, rows, width), jnp.bfloat16),
+                        pltpu.VMEM((XN, rows, width), jnp.bfloat16),
+                        pltpu.VMEM((n // XN, rows, width), jnp.bfloat16),
+                        pltpu.SemaphoreType.DMA((copies,)), pltpu.SemaphoreType.DMA((copies,))],
+        compiler_params=pltpu.CompilerParams(collective_id=1, has_side_effects=True, vmem_limit_bytes=48 << 20),
+        name="scatter",
+    )(ck, cv, gk, gv)
+
+
+def copies_of(n):
+    total = 0
+    for na, nb in ((XN, n // XN), (n // XN, XN)):
+        total += 2 * (na // 2) + na * 2 * (nb // 2)
+    return total
 
 
 def local(queries, keys, values, grad_out, key_blocks, key_count):
-    rows = queries.shape[0]
+    n = lax.axis_size("ctx")
+    rows = keys.shape[0]
     pos = lax.axis_index("ctx").astype(jnp.int32).reshape(1)
-    own = jnp.concatenate([keys, values], axis=1)
-    every = lax.all_gather(own, "ctx", axis=0, tiled=True).reshape(-1, BLOCK, 2 * DH)
-    att, gq, gown, contrib = attention(key_blocks.reshape(-1), key_count, pos, queries, grad_out, own, every)
-    mine = lax.psum_scatter(contrib, "ctx", scatter_dimension=0, tiled=True)
-    total = (gown + mine.reshape(rows, 2 * DH).astype(jnp.float32)).astype(jnp.bfloat16)
-    return att, gq, total[:, :DH], total[:, DH:]
+    copies = copies_of(n)
+    k_all, v_all = gather(n, keys, values, copies)
+    k_all, v_all = (a.reshape(-1, BLOCK, DH) for a in (k_all, v_all))
+    att, gq, gk, gv, ck, cv = attention(
+        key_blocks.reshape(-1), key_count, pos, queries, grad_out, keys, values, k_all, v_all)
+    grad_k, grad_v = scatter(n, ck.reshape(n, rows, DH), cv.reshape(n, rows, DH), gk, gv, copies)
+    return att, gq, grad_k, grad_v
 
 
 def solution(mesh):

time: 341 us -> 90.9 us (0.27)
  waiting for transfers between devices: 304 us -> 0 us
  Pallas kernels: 11.6 us -> 83.2 us
  between operations: 14.1 us -> 0.67 us
    reduce_scatter x1 -> x0, waiting for transfers between devices: 219 us -> none  [local(): mine = lax.psum_scatter(contrib, 'ctx', scatter_dimension=0, tiled=True)]
    all_gather x1 -> x0, waiting for transfers between devices: 85.3 us -> none  [local(): lax.all_gather(own, 'ctx', axis=0, tiled=True).reshape(-1, BLOCK, 2 * DH)]
    pallas_call x1 -> x3, Pallas kernels: 11.6 us -> 83.2 us  [the longest x1 39.9 us: gather(): pl.pallas_call(functools.partial(gather_kernel, n), out_shape=[shape, sha...]
    unnamed x14 -> x13, local copies, waits for them, and re-layouts: 7.88 us -> 6.45 us
  transfers between devices with their start and end apart: 2 -> 0, of which waited for: 2 -> 0; matrix products, arithmetic and copies ran while one was open for 0% -> 0% of each run, Pallas kernels for 0% -> 0%
where the time goes in v2:
time: 90.9 us; the launch traced here: 90.5 us
  Pallas kernels  83.2 us (92%)
  local copies, waits for them, and re-layouts  6.58 us (7%)
    pallas_call x1, Pallas kernels, gather(): pl.pallas_call(functools.partial(gather_kernel, n), out_shape=[shape, sha...  39.9 us
    pallas_call x1, Pallas kernels, scatter(): pl.pallas_call(functools.partial(scatter_kernel, n), out_shape=[shape, sh...  31.2 us
    pallas_call x1, Pallas kernels, attention(): pl.pallas_call(attn_kernel, grid_spec=spec, out_shape=[out((rows, width),...  12.2 us
    unnamed x13, local copies, waits for them, and re-layouts  6.45 us

profile of v2, /device:TPU:8, one launch (start us, length us, event | category | flops | bytes accessed | tf_op | source)
XLA Modules:
  0.0 90.5 jit_solution(12984943811701470320)
XLA Ops:
  0.6 0.8 copy.10
  1.4 0.1 reshape.26.kb
  1.6 39.9 %gather.1 = (bf16[32,256,128]{2,1,0:T(8,128)(2,1)}, bf16[32,256,128]{2,1,0:T(8,128)(2,1)}) custom-call(bf16[256,128]{1,0:T(8,128)(2,1)} %k_own.1, bf16[256,128]{1,0:T(8,128)(2,1)} %v_own.1), custom_call_target="tpu_custom_call" | custom-call | tf_op jit(solution)/shard_map/gather/pallas_call | solution.py:268
  41.5 0.0 copy-start
  41.5 1.0 %copy-done = bf16[256,1024]{1,0:T(8,128)(2,1)S(1)} copy-done((bf16[256,1024]{1,0:T(8,128)(2,1)S(1)}, bf16[256,1024]{1,0:T(8,128)(2,1)}, u32[]{:S(2)}) %copy-start) | copy-done | bytes 524312
  42.5 0.0 copy-start.1
  42.5 1.0 %copy-done.1 = bf16[256,1024]{1,0:T(8,128)(2,1)S(1)} copy-done((bf16[256,1024]{1,0:T(8,128)(2,1)S(1)}, bf16[256,1024]{1,0:T(8,128)(2,1)}, u32[]{:S(2)}) %copy-start.1) | copy-done | bytes 524312
  43.5 0.0 copy-start.2
  43.5 0.8 copy-done.2
  44.4 0.0 copy-start.3
  44.4 0.8 copy-done.3
  45.2 0.0 copy-start.4
  45.2 0.7 copy-done.4
  45.9 12.2 %attention.1 = (bf16[256,1024]{1,0:T(8,128)(2,1)}, bf16[256,1024]{1,0:T(8,128)(2,1)}, f32[256,128]{1,0:T(8,128)S(1)}, f32[256,128]{1,0:T(8,128)S(1)}, bf16[64,12...) custom-call(s32[384]{0:T(512)S(1)} %reshape.26.kb, s32[64]{0:T(128)S(1)} %copy-done.4, s32[1]{0:T(128)} %bitcast.pos, ...), custom_call_target="tpu_custom_call" | custom-call | tf_op jit(solution)/shard_map/attention/pallas_call | solution.py:136
  58.0 31.2 %scatter.1 = (bf16[256,128]{1,0:T(8,128)(2,1)S(1)}, bf16[256,128]{1,0:T(8,128)(2,1)S(1)}) custom-call(bf16[32,256,128]{2,1,0:T(8,128)(2,1)S(1)} %bitcast.5, bf16[32,256,128]{2,1,0:T(8,128)(2,1)S(1)} %bitcast.6, f32[256,128]{1,0:T(8,128)S(1)} %get-tuple-element.20.gk_ref, f32[256,128]{1,0:T(8,128)S(1)} %get-tuple-element.21.gv_ref), custom_call_target="tpu_custom_call" | custom-call | tf_op jit(solution)/shard_map/scatter/pallas_call | solution.py:390
  89.2 0.6 copy.13
  89.9 0.6 copy.14
Async XLA Ops:
  41.5 1.0 %copy-start = (bf16[256,1024]{1,0:T(8,128)(2,1)S(1)}, bf16[256,1024]{1,0:T(8,128)(2,1)}, u32[]{:S(2)}) copy-start(bf16[256,1024]{1,0:T(8,128)(2,1)} %q_ref.1) | copy-start | bytes 1572868
  42.5 1.0 %copy-start.1 = (bf16[256,1024]{1,0:T(8,128)(2,1)S(1)}, bf16[256,1024]{1,0:T(8,128)(2,1)}, u32[]{:S(2)}) copy-start(bf16[256,1024]{1,0:T(8,128)(2,1)} %o_ref.1) | copy-start | bytes 1572868
  43.5 0.8 copy-start.2
  44.4 0.8 copy-start.3
  45.2 0.7 copy-start.4

commit v3 on v1

v3 whole, which is shorter than its diff:
```python
import functools
import math

import jax
import jax.numpy as jnp
from jax import lax
from jax.experimental import pallas as pl
from jax.experimental.pallas import tpu as pltpu
from jax.sharding import PartitionSpec as P

QH = 64
KVH = 8
DH = 128
BLOCK = 128
KSLOTS = 6
NSLOT = KSLOTS + 1
GROUP = QH // KVH
BLK_DEV = 2
ENTRIES = BLK_DEV * KSLOTS
XN = 4
ZN = 8
HALF = BLOCK // 2
FAR = (XN - 1) * ZN
WIDE = NSLOT * BLOCK
SCALING = 1.0 / math.sqrt(DH)
SCALE2 = SCALING * 1.4426950408889634
NEG = -1e30
COPIES = 160
MESH = pl.DeviceIdType.MESH
BF16 = jnp.bfloat16
F32 = jnp.float32
NT = (((1,), (1,)), ((), ()))


def place(u):
    return 0 if u == 0 else (2 * u - 1 if u <= ZN // 2 else 2 * (ZN - u))


GROUPS = [(0, 1)] + [(2 * t - 1, 2) for t in range(1, ZN // 2)] + [(ZN - 1, 1)]
RANGE_AT = sorted(range(ZN), key=place)


def kernel(kb, kc, q_hbm, o_hbm, k_hbm, v_hbm, att_hbm, gq_hbm, outk_ref, outv_ref,
           q_in, o_in, att_s, gq_s, near_k, near_v, stage, transit, terms, ring, rowsum,
           parts_k, parts_v, own_k, own_v, k_s, v_s, kt_s, vt_s, q_st, o_st, e_s, p_s, ds_s, inv_s,
           which_s, slot_s, load_s, send_sem, recv_sem, local_sem):
    position = lax.axis_index("ctx")
    x = lax.rem(position, XN)
    z = lax.div(position, XN)
    near = [near_k, near_v]
    kv_hbm = [k_hbm, v_hbm]

    def along_x(dx):
        return z * XN + lax.rem(x + dx % XN, XN)

    def along_z(dz):
        return lax.rem(z + dz % ZN, ZN) * XN + x

    barrier = pltpu.get_barrier_semaphore()
    for d in (1, -1):
        pl.semaphore_signal(barrier, inc=1, device_id={"ctx": along_x(d)}, device_id_type=MESH)
        pl.semaphore_signal(barrier, inc=1, device_id={"ctx": along_z(d)}, device_id_type=MESH)

    loads = []
    for i, (src, dst) in enumerate((
            (k_hbm, near_k.at[pl.ds(FAR, BLK_DEV)]), (v_hbm, near_v.at[pl.ds(FAR, BLK_DEV)]),
            (q_hbm, q_in), (o_hbm, o_in))):
        copy = pltpu.make_async_copy(src, dst, local_sem.at[i])
        copy.start()
        loads.append(copy)

    for dx in range(XN):
        reader = along_x(dx) * BLK_DEV
        blocks, owners = [], []
        for e in range(ENTRIES):
            block = kb[reader + e // KSLOTS, e % KSLOTS]
            live = e % KSLOTS < kc[reader + e // KSLOTS]
            blocks.append(lax.rem(block, BLK_DEV))
            owners.append(jnp.where(live, lax.div(block, BLK_DEV), -1))
        for u in range(ZN):
            wanted = along_z(u)
            which = jnp.int32(0)
            for e in range(ENTRIES):
                which = jnp.where(owners[e] == wanted, blocks[e], which)
            which_s[dx * ZN + u] = which
        if dx == 0:
            for ax in range(XN):
                for u in range(ZN):
                    wanted = lax.rem(z + u, ZN) * XN + lax.rem(x + ax, XN)
                    slot = jnp.int32(ENTRIES)
                    for e in range(ENTRIES):
                        slot = jnp.where(owners[e] == wanted, e, slot)
                    slot_s[ax * ZN + u] = slot
    for b in range(BLK_DEV):
        block = position * BLK_DEV + b
        first = None
        for s in range(KSLOTS):
            listed = kb[block, s]
            owner = lax.div(listed, BLK_DEV)
            dx = lax.rem(lax.rem(owner, XN) - x + XN, XN)
            u = lax.rem(lax.div(owner, XN) - z + ZN, ZN)
            spot = jnp.where(u == 0, 0, jnp.where(u <= ZN // 2, 2 * u - 1, 2 * (ZN - u)))
            at = jnp.where(dx == 0, FAR + BLK_DEV * u + lax.rem(listed, BLK_DEV), (dx - 1) * ZN + spot)
            first = at if s == 0 else first
            load_s[b * KSLOTS + s] = jnp.where(s < kc[block], at, first)

    used = [0]
    sent = []

    def send(src, dst, device):
        at = used[0]
        used[0] += 1
        copy = pltpu.make_async_remote_copy(
            src_ref=src, dst_ref=dst, send_sem=send_sem.at[at], recv_sem=recv_sem.at[at],
            device_id={"ctx": device}, device_id_type=MESH)
        copy.start()
        sent.append(copy)
        return copy

    def column(i, u, t, d):
        first = FAR + BLK_DEV * (u % ZN)
        if 2 * t < ZN:
            return near[i].at[pl.ds(first, BLK_DEV)]
        return near[i].at[pl.ds(first + (0 if d == 1 else 1), 1)]

    def ring_send(i, t):
        out = []
        for d in (1, -1):
            u = -d * (t - 1)
            if t > 1:
                src = column(i, u, t, d)
            else:
                src = kv_hbm[i]
            out.append(send(src, column(i, u - d, t, d), along_z(d)))
        return out

    def spread(phase, group, dst):
        first, count = group
        here = pl.ds(first, count)
        out = []
        for d in (1, -1):
            a = (d - 1) % XN
            b = (-d - 1) % XN
            straight = send(stage.at[phase, pl.ds(a * ZN + first, count)], dst.at[pl.ds(b * ZN + first, count)], along_x(d))
            rows = pl.ds(0 if d == 1 else HALF, HALF)
            through = send(stage.at[phase, pl.ds(ZN + first, count), rows], transit.at[phase, 0 if d == 1 else 1, here], along_x(d))
            out.append((d, straight, through))
        return out

    def forward(phase, group, moves, dst):
        first, count = group
        out = []
        for d, straight, through in moves:
            through.wait_recv()
            rows = pl.ds(0 if d == 1 else HALF, HALF)
            out.append(send(transit.at[phase, 0 if d == 1 else 1, pl.ds(first, count)], dst.at[pl.ds(ZN + first, count), rows], along_x(d)))
        return out

    def arrive(moves, passed):
        for _, straight, _ in moves:
            straight.wait_recv()
        for copy in passed:
            copy.wait_recv()

    def choose(i, group):
        first, count = group
        for j in range(first, first + count):
            u = RANGE_AT[j]
            low, high = near[i][FAR + BLK_DEV * u], near[i][FAR + BLK_DEV * u + 1]
            for dx in range(1, XN):
                stage[i, (dx - 1) * ZN + j] = jnp.where(which_s[dx * ZN + u] == 1, high, low)

    pl.semaphore_wait(barrier, 4)

    top = ZN // 2
    moves = [[None] * len(GROUPS) for _ in range(4)]
    passed = [[None] * len(GROUPS) for _ in range(4)]

    def gather_x(i, t):
        choose(i, GROUPS[t])
        moves[i][t] = spread(i, GROUPS[t], near[i])

    def gather_on(i, t):
        passed[i][t] = forward(i, GROUPS[t], moves[i][t], near[i])

    rings = [None, None]

    def ring_step(i, t):
        for copy in rings[i]:
            copy.wait_recv()
        rings[i] = ring_send(i, t + 1) if t < top else None

    rings[0] = ring_send(0, 1)
    loads[0].wait()
    gather_x(0, 0)
    for t in range(1, top + 1):
        ring_step(0, t)
        gather_x(0, t)
        if t == 2:
            rings[1] = ring_send(1, 1)
        if t > 2:
            ring_step(1, t - 2)
        gather_on(0, t - 1)
    gather_on(0, top)
    ring_step(1, top - 1)
    loads[1].wait()
    for t in range(top):
        gather_x(1, t)
    ring_step(1, top)
    gather_x(1, top)
    loads[2].wait()
    loads[3].wait()
    for t in range(top + 1):
        arrive(moves[0][t], passed[0][t])

    def rows_of(s):
        return pl.ds(s * BLOCK, BLOCK)

    def fetch(i, b):
        full, turned = (k_s, kt_s) if i == 0 else (v_s, vt_s)
        for s in range(NSLOT):
            at = FAR + b if s == 0 else load_s[b * KSLOTS + s - 1]
            block = near[i][at]
            full[b, rows_of(s), :] = block
            turned[b, :, rows_of(s)] = block.T

    def bias(b, s):
        return jnp.where(s < kc[position * BLK_DEV + b], 0.0, NEG).astype(F32)

    def probs(b, pair):
        cols = pl.ds(pair * 2 * BLOCK, 2 * BLOCK)
        for h in (2 * pair, 2 * pair + 1):
            q_st[b, pl.ds(h * BLOCK, BLOCK), :] = q_in[b, :, pl.ds(h * DH, DH)]
            o_st[b, pl.ds(h * BLOCK, BLOCK), :] = o_in[b, :, pl.ds(h * DH, DH)]
        q2 = q_st[b, cols, :]
        m = None
        for s in range(NSLOT):
            sc = lax.dot_general(k_s[b, rows_of(s), :], q2, NT, preferred_element_type=F32)
            e_s[b, rows_of(s), cols] = sc
            high = jnp.max(sc, axis=0, keepdims=True)
            if s > 0:
                high = high + bias(b, s - 1)
            m = high if m is None else jnp.maximum(m, high)
        mc = m * SCALE2
        total = None
        for s in range(NSLOT):
            off = -mc if s == 0 else bias(b, s - 1) - mc
            e = jnp.exp2(e_s[b, rows_of(s), cols] * SCALE2 + off)
            e_s[b, rows_of(s), cols] = e
            part = jnp.sum(e, axis=0, keepdims=True)
            total = part if total is None else total + part
        inv = 1.0 / total
        inv_s[b, :, cols] = jnp.broadcast_to(inv, (8, 2 * BLOCK))
        for s in range(NSLOT):
            p_s[b, rows_of(s), cols] = (e_s[b, rows_of(s), cols] * inv).astype(BF16)

    def key_side(b, weights, rows_in, parts, own):
        for s in range(NSLOT):
            g = jnp.dot(weights[b, rows_of(s), :], rows_in[b], preferred_element_type=F32)
            if s == 0:
                own[b] = g
            else:
                parts[b * KSLOTS + s - 1] = g.astype(BF16)

    def query_side(b, pair):
        cols = pl.ds(pair * 2 * BLOCK, 2 * BLOCK)
        o2 = o_st[b, cols, :]
        out_t = jnp.dot(vt_s[b], p_s[b, :, cols], preferred_element_type=F32)
        att_t = out_t.astype(BF16)
        delta = jnp.sum(o2.T.astype(F32) * att_t.astype(F32), axis=0, keepdims=True)
        inv = inv_s[b, pl.ds(0, 1), cols] * SCALING
        for s in range(NSLOT):
            dp = lax.dot_general(v_s[b, rows_of(s), :], o2, NT, preferred_element_type=F32)
            ds_s[b, rows_of(s), cols] = ((e_s[b, rows_of(s), cols] * inv) * (dp - delta)).astype(BF16)
        gq_t = jnp.dot(kt_s[b], ds_s[b, :, cols], preferred_element_type=F32).astype(BF16)
        att, gq = att_t.T, gq_t.T
        for j in (0, 1):
            h = pl.ds((2 * pair + j) * DH, DH)
            att_s[b, :, h] = att[j * BLOCK:(j + 1) * BLOCK]
            gq_s[b, :, h] = gq[j * BLOCK:(j + 1) * BLOCK]

    parts = [parts_k, parts_v]

    def scatter_x(i, t):
        first, count = GROUPS[t]
        for j in range(first, first + count):
            for dx in range(1, XN):
                stage[2 + i, (dx - 1) * ZN + j] = parts[i][slot_s[dx * ZN + RANGE_AT[j]]]
        moves[2 + i][t] = spread(2 + i, GROUPS[t], terms.at[i])

    def scatter_on(i, t):
        passed[2 + i][t] = forward(2 + i, GROUPS[t], moves[2 + i][t], terms.at[i])

    def row_sums(i, t):
        arrive(moves[2 + i][t], passed[2 + i][t])
        first, count = GROUPS[t]
        for j in range(first, first + count):
            u = RANGE_AT[j]
            low = high = None
            for dx in range(XN):
                if dx == 0 and u == 0:
                    continue
                if dx == 0:
                    term = parts[i][slot_s[u]].astype(F32)
                else:
                    term = terms[i, (dx - 1) * ZN + j].astype(F32)
                second = which_s[dx * ZN + u] == 1
                up = jnp.where(second, term, 0.0)
                down = jnp.where(second, 0.0, term)
                high = up if high is None else high + up
                low = down if low is None else low + down
            rowsum[i, u, 0] = low.astype(BF16)
            rowsum[i, u, 1] = high.astype(BF16)

    chains = [None, None]

    def chain(i, t):
        out = []
        for j, d in enumerate((1, -1)):
            u = (-d * t) % ZN
            half = pl.ds(0 if d == 1 else 1, 1)
            if t == top:
                src, dst = rowsum.at[i, u, half], ring.at[i, j, t - 1, half]
            else:
                chains[i][j].wait_recv()
                for w in range(BLK_DEV):
                    if t + 1 < top or w == j:
                        both = rowsum[i, u, w].astype(F32) + ring[i, j, t, w].astype(F32)
                        rowsum[i, u, w] = both.astype(BF16)
                src, dst = rowsum.at[i, u], ring.at[i, j, t - 1]
            out.append(send(src, dst, along_z(-d)))
        chains[i] = out

    def finish(i):
        for copy in chains[i]:
            copy.wait_recv()
        own = (own_k, own_v)[i]
        out = (outk_ref, outv_ref)[i]
        for w in range(BLK_DEV):
            total = own[w] + rowsum[i, 0, w].astype(F32)
            total = total + ring[i, 0, 0, w].astype(F32) + ring[i, 1, 0, w].astype(F32)
            out[w] = total.astype(BF16)

    pairs = GROUP // 2
    units = [(b, pair) for b in range(BLK_DEV) for pair in range(pairs)]
    for i in (0, 1):
        parts[i][ENTRIES] = jnp.zeros((BLOCK, DH), BF16)
    for n, (b, pair) in enumerate(units):
        if pair == 0:
            fetch(0, b)
        probs(b, pair)
        if n <= top:
            gather_on(1, n)
        if pair == pairs - 1:
            key_side(b, p_s, o_st, parts_v, own_v)
    for t in range(top, -1, -1):
        scatter_x(1, t)
    for t in range(top + 1):
        arrive(moves[1][t], passed[1][t])
    stores = []
    for n, (b, pair) in enumerate(units):
        if pair == 0:
            fetch(1, b)
        query_side(b, pair)
        if n <= top:
            scatter_on(1, top - n)
        if n > 2:
            row_sums(1, top + 3 - n)
            if n - 3 < top:
                chain(1, top + 3 - n)
        if pair == pairs - 1:
            key_side(b, ds_s, q_st, parts_k, own_k)
            for src, dst in ((att_s, att_hbm), (gq_s, gq_hbm)):
                copy = pltpu.make_async_copy(src.at[b], dst.at[b], local_sem.at[4 + len(stores)])
                copy.start()
                stores.append(copy)
    for t in range(top, -1, -1):
        scatter_x(0, t)
    done = len(units) - 3
    for t in range(top, -1, -1):
        scatter_on(0, t)
        if top - t >= done:
            row_sums(1, t)
    for t in range(top - done, -1, -1):
        if t > 0 and top - t >= done:
            chain(1, t)
    for t in range(top, -1, -1):
        row_sums(0, t)
        if t > 0:
            chain(0, t)
    finish(1)
    finish(0)
    for copy in sent:
        copy.wait_send()
    for copy in stores:
        copy.wait()


def local(queries, keys, values, grad_out, key_blocks, key_count):
    rows, width = queries.shape
    wide = (BLK_DEV, BLOCK, width)
    own = (BLK_DEV, BLOCK, DH)
    any_spec = pl.BlockSpec(memory_space=pl.ANY)
    smem_spec = pl.BlockSpec(memory_space=pltpu.SMEM)
    vmem_spec = pl.BlockSpec(memory_space=pltpu.VMEM)
    vmem = pltpu.VMEM
    att, gq, gk, gv = pl.pallas_call(
        kernel,
        out_shape=[jax.ShapeDtypeStruct(wide, BF16)] * 2 + [jax.ShapeDtypeStruct(own, BF16)] * 2,
        in_specs=[smem_spec] * 2 + [any_spec] * 4,
        out_specs=[any_spec] * 2 + [vmem_spec] * 2,
        scratch_shapes=[
            vmem(wide, BF16), vmem(wide, BF16), vmem(wide, BF16), vmem(wide, BF16),
            vmem((FAR + BLK_DEV * ZN, BLOCK, DH), BF16), vmem((FAR + BLK_DEV * ZN, BLOCK, DH), BF16),
            vmem((4, FAR, BLOCK, DH), BF16), vmem((4, 2, ZN, HALF, DH), BF16), vmem((2, FAR, BLOCK, DH), BF16),
            vmem((2, 2, ZN // 2, BLK_DEV, BLOCK, DH), BF16), vmem((2, ZN, BLK_DEV, BLOCK, DH), BF16),
            vmem((ENTRIES + 1, BLOCK, DH), BF16), vmem((ENTRIES + 1, BLOCK, DH), BF16),
            vmem(own, F32), vmem(own, F32),
            vmem((BLK_DEV, WIDE, DH), BF16), vmem((BLK_DEV, WIDE, DH), BF16),
            vmem((BLK_DEV, DH, WIDE), BF16), vmem((BLK_DEV, DH, WIDE), BF16),
            vmem((BLK_DEV, GROUP * BLOCK, DH), BF16), vmem((BLK_DEV, GROUP * BLOCK, DH), BF16),
            vmem((BLK_DEV, WIDE, GROUP * BLOCK), F32),
            vmem((BLK_DEV, WIDE, GROUP * BLOCK), BF16), vmem((BLK_DEV, WIDE, GROUP * BLOCK), BF16),
            vmem((BLK_DEV, 8, GROUP * BLOCK), F32),
            pltpu.SMEM((XN * ZN,), jnp.int32), pltpu.SMEM((XN * ZN,), jnp.int32), pltpu.SMEM((ENTRIES,), jnp.int32),
            pltpu.SemaphoreType.DMA((COPIES,)), pltpu.SemaphoreType.DMA((COPIES,)), pltpu.SemaphoreType.DMA((8,))],
        compiler_params=pltpu.CompilerParams(collective_id=0, has_side_effects=True, vmem_limit_bytes=56 << 20),
        name="sparse_attention",
    )(key_blocks, key_count, queries.reshape(wide), grad_out.reshape(wide), keys.reshape(own), values.reshape(own))
    return att.reshape(rows, width), gq.reshape(rows, width), gk.reshape(rows, DH), gv.reshape(rows, DH)


def solution(mesh):
    in_specs = (P("ctx", "head"), P("ctx", "head"), P("ctx", "head"), P("ctx", "head"), P(), P())
    out_specs = (P("ctx", "head"), P("ctx", "head"), P("ctx", "head"), P("ctx", "head"))
    return jax.shard_map(local, mesh=mesh, in_specs=in_specs, out_specs=out_specs, check_vma=False)
```

time: 341 us -> 94.3 us (0.28)
  waiting for transfers between devices: 304 us -> 0 us
  Pallas kernels: 11.6 us -> 87.7 us
  between operations: 14.1 us -> 0.66 us
  local copies, waits for them, and re-layouts: 9.53 us -> 5.67 us
    reduce_scatter x1 -> x0, waiting for transfers between devices: 219 us -> none  [local(): mine = lax.psum_scatter(contrib, 'ctx', scatter_dimension=0, tiled=True)]
    all_gather x1 -> x0, waiting for transfers between devices: 85.3 us -> none  [local(): lax.all_gather(own, 'ctx', axis=0, tiled=True).reshape(-1, BLOCK, 2 * DH)]
    pallas_call x1, Pallas kernels: 11.6 us -> 87.7 us  [local(): pl.pallas_call(kernel, out_shape=[jax.ShapeDtypeStruct(wide, BF16)] * 2 +...]
    unnamed x14 -> x13, local copies, waits for them, and re-layouts: 7.88 us -> 5.67 us
  transfers between devices with their start and end apart: 2 -> 0, of which waited for: 2 -> 0; matrix products, arithmetic and copies ran while one was open for 0% -> 0% of each run, Pallas kernels for 0% -> 0%
where the time goes in v3:
time: 94.3 us; the launch traced here: 94 us
  Pallas kernels  87.7 us (93%)
  local copies, waits for them, and re-layouts  5.67 us (6%)
    pallas_call x1, Pallas kernels, local(): pl.pallas_call(kernel, out_shape=[jax.ShapeDtypeStruct(wide, BF16)] * 2 +...  87.7 us
    unnamed x13, local copies, waits for them, and re-layouts  5.67 us

profile of v3, /device:TPU:8, one launch (start us, length us, event | category | flops | bytes accessed | tf_op | source)
XLA Modules:
  0.0 94.0 jit_solution(3695673970022902759)
XLA Ops:
  0.6 0.0 copy-start.3
  0.6 0.7 copy-done.3
  1.3 0.7 copy.10.kb
  2.0 87.7 %sparse_attention.1 = (bf16[2,128,1024]{2,1,0:T(8,128)(2,1)}, bf16[2,128,1024]{2,1,0:T(8,128)(2,1)}, bf16[2,128,128]{2,1,0:T(8,128)(2,1)}, bf16[2,128,128]{2,1,0:T(8,128)(2,1)}) custom-call(s32[64,6]{1,0:T(8,128)} %copy.10.kb, s32[64]{0:T(128)} %kc.1, bf16[2,128,1024]{2,1,0:T(8,128)(2,1)} %bitcast.8, bf16[2,128,1024]{2,1,0:T(8,128)(2,1)} %bitcast.9, ...), custom_call_target="tpu_custom_call" | custom-call | tf_op jit(solution)/shard_map/sparse_attention/pallas_call | solution.py:407
  89.7 0.0 copy-start
  89.7 1.9 %copy.15 = bf16[256,1024]{1,0:T(8,128)(2,1)} copy(bf16[256,1024]{1,0:T(8,128)(2,1)} %bitcast.11) | data formatting | bytes 1048576
  91.6 0.0 copy-done
  91.6 0.0 copy-start.2
  91.6 0.8 copy.16
  92.4 0.1 copy-done.2
  92.5 0.0 copy-start.1
  92.5 0.6 copy.17
  93.1 0.2 copy-done.1
  93.4 0.6 copy.18
Async XLA Ops:
  0.6 0.7 copy-start.3
  89.7 1.9 %copy-start = (bf16[2,128,1024]{2,1,0:T(8,128)(2,1)S(1)}, bf16[2,128,1024]{2,1,0:T(8,128)(2,1)}, u32[]{:S(2)}) copy-start(bf16[2,128,1024]{2,1,0:T(8,128)(2,1)} %get-tuple-element.9) | copy-start | bytes 1572868
  91.6 0.9 copy-start.2
  92.5 0.9 copy-start.1

commit v4 on v3

--- a/solution.py
+++ b/solution.py
@@ -19,7 +19,6 @@
 ENTRIES = BLK_DEV * KSLOTS
 XN = 4
 ZN = 8
-HALF = BLOCK // 2
 FAR = (XN - 1) * ZN
 WIDE = NSLOT * BLOCK
 SCALING = 1.0 / math.sqrt(DH)
@@ -41,8 +40,8 @@
 
 
 def kernel(kb, kc, q_hbm, o_hbm, k_hbm, v_hbm, att_hbm, gq_hbm, outk_ref, outv_ref,
-           q_in, o_in, att_s, gq_s, near_k, near_v, stage, transit, terms, ring, rowsum,
-           parts_k, parts_v, own_k, own_v, k_s, v_s, kt_s, vt_s, q_st, o_st, e_s, p_s, ds_s, inv_s,
+           q_in, o_in, att_s, gq_s, near_k, near_v, stage, terms, ring, rowsum,
+           parts_k, parts_v, own_k, own_v, k_s, v_s, kt_s, vt_s, q_st, o_st, e_s, p_s, ds_s, dp_s, inv_s,
            which_s, slot_s, load_s, send_sem, recv_sem, local_sem):
     position = lax.axis_index("ctx")
     x = lax.rem(position, XN)
@@ -57,9 +56,9 @@
         return lax.rem(z + dz % ZN, ZN) * XN + x
 
     barrier = pltpu.get_barrier_semaphore()
-    for d in (1, -1):
-        pl.semaphore_signal(barrier, inc=1, device_id={"ctx": along_x(d)}, device_id_type=MESH)
-        pl.semaphore_signal(barrier, inc=1, device_id={"ctx": along_z(d)}, device_id_type=MESH)
+    partners = [along_x(d) for d in range(1, XN)] + [along_z(d) for d in (1, -1, 2, -2)]
+    for partner in partners:
+        pl.semaphore_signal(barrier, inc=1, device_id={"ctx": partner}, device_id_type=MESH)
 
     loads = []
     for i, (src, dst) in enumerate((
@@ -117,49 +116,28 @@
         sent.append(copy)
         return copy
 
-    def column(i, u, t, d):
+    def column(i, u, half=None):
         first = FAR + BLK_DEV * (u % ZN)
-        if 2 * t < ZN:
+        if half is None:
             return near[i].at[pl.ds(first, BLK_DEV)]
-        return near[i].at[pl.ds(first + (0 if d == 1 else 1), 1)]
-
-    def ring_send(i, t):
-        out = []
-        for d in (1, -1):
-            u = -d * (t - 1)
-            if t > 1:
-                src = column(i, u, t, d)
-            else:
-                src = kv_hbm[i]
-            out.append(send(src, column(i, u - d, t, d), along_z(d)))
+        return near[i].at[pl.ds(first + half, 1)]
+
+    def ring_near(i):
+        return {(t, d): send(kv_hbm[i], column(i, -d * t), along_z(d * t)) for t in (1, 2) for d in (1, -1)}
+
+    def ring_far(i):
+        out = {(3, d): send(column(i, -2 * d), column(i, -3 * d), along_z(d)) for d in (1, -1)}
+        for half, d in enumerate((1, -1)):
+            out[4, d] = send(column(i, -2 * d, half), column(i, 4, half), along_z(2 * d))
         return out
 
     def spread(phase, group, dst):
         first, count = group
-        here = pl.ds(first, count)
-        out = []
-        for d in (1, -1):
-            a = (d - 1) % XN
-            b = (-d - 1) % XN
-            straight = send(stage.at[phase, pl.ds(a * ZN + first, count)], dst.at[pl.ds(b * ZN + first, count)], along_x(d))
-            rows = pl.ds(0 if d == 1 else HALF, HALF)
-            through = send(stage.at[phase, pl.ds(ZN + first, count), rows], transit.at[phase, 0 if d == 1 else 1, here], along_x(d))
-            out.append((d, straight, through))
-        return out
-
-    def forward(phase, group, moves, dst):
-        first, count = group
-        out = []
-        for d, straight, through in moves:
-            through.wait_recv()
-            rows = pl.ds(0 if d == 1 else HALF, HALF)
-            out.append(send(transit.at[phase, 0 if d == 1 else 1, pl.ds(first, count)], dst.at[pl.ds(ZN + first, count), rows], along_x(d)))
-        return out
-
-    def arrive(moves, passed):
-        for _, straight, _ in moves:
-            straight.wait_recv()
-        for copy in passed:
+        return [send(stage.at[phase, pl.ds((dx - 1) * ZN + first, count)],
+                     dst.at[pl.ds((XN - dx - 1) * ZN + first, count)], along_x(dx)) for dx in (2, 1, 3)]
+
+    def arrive(copies):
+        for copy in copies:
             copy.wait_recv()
 
     def choose(i, group):
@@ -170,48 +148,48 @@
             for dx in range(1, XN):
                 stage[i, (dx - 1) * ZN + j] = jnp.where(which_s[dx * ZN + u] == 1, high, low)
 
-    pl.semaphore_wait(barrier, 4)
+    pl.semaphore_wait(barrier, len(partners))
 
     top = ZN // 2
     moves = [[None] * len(GROUPS) for _ in range(4)]
-    passed = [[None] * len(GROUPS) for _ in range(4)]
+    rings = [{}, {}]
 
     def gather_x(i, t):
         choose(i, GROUPS[t])
         moves[i][t] = spread(i, GROUPS[t], near[i])
 
-    def gather_on(i, t):
-        passed[i][t] = forward(i, GROUPS[t], moves[i][t], near[i])
-
-    rings = [None, None]
-
-    def ring_step(i, t):
-        for copy in rings[i]:
-            copy.wait_recv()
-        rings[i] = ring_send(i, t + 1) if t < top else None
-
-    rings[0] = ring_send(0, 1)
+    def come(i, t):
+        for d in (1, -1):
+            rings[i][t, d].wait_recv()
+
+    rings[0].update(ring_near(0))
     loads[0].wait()
     gather_x(0, 0)
-    for t in range(1, top + 1):
-        ring_step(0, t)
-        gather_x(0, t)
-        if t == 2:
-            rings[1] = ring_send(1, 1)
-        if t > 2:
-            ring_step(1, t - 2)
-        gather_on(0, t - 1)
-    gather_on(0, top)
-    ring_step(1, top - 1)
+    rings[1].update(ring_near(1))
+    come(0, 1)
+    gather_x(0, 1)
+    come(0, 2)
+    rings[0].update(ring_far(0))
+    gather_x(0, 2)
     loads[1].wait()
-    for t in range(top):
-        gather_x(1, t)
-    ring_step(1, top)
-    gather_x(1, top)
+    gather_x(1, 0)
+    come(1, 1)
+    gather_x(1, 1)
+    come(1, 2)
+    rings[1].update(ring_far(1))
+    come(0, 3)
+    gather_x(0, 3)
+    come(0, 4)
+    gather_x(0, 4)
+    gather_x(1, 2)
+    come(1, 3)
+    gather_x(1, 3)
+    come(1, 4)
+    gather_x(1, 4)
     loads[2].wait()
     loads[3].wait()
     for t in range(top + 1):
-        arrive(moves[0][t], passed[0][t])
+        arrive(moves[0][t])
 
     def rows_of(s):
         return pl.ds(s * BLOCK, BLOCK)
@@ -234,10 +212,9 @@
             o_st[b, pl.ds(h * BLOCK, BLOCK), :] = o_in[b, :, pl.ds(h * DH, DH)]
         q2 = q_st[b, cols, :]
         m = None
+        e_s[b, :, cols] = lax.dot_general(k_s[b], q2, NT, preferred_element_type=F32)
         for s in range(NSLOT):
-            sc = lax.dot_general(k_s[b, rows_of(s), :], q2, NT, preferred_element_type=F32)
-            e_s[b, rows_of(s), cols] = sc
-            high = jnp.max(sc, axis=0, keepdims=True)
+            high = jnp.max(e_s[b, rows_of(s), cols], axis=0, keepdims=True)
             if s > 0:
                 high = high + bias(b, s - 1)
             m = high if m is None else jnp.maximum(m, high)
@@ -255,22 +232,21 @@
             p_s[b, rows_of(s), cols] = (e_s[b, rows_of(s), cols] * inv).astype(BF16)
 
     def key_side(b, weights, rows_in, parts, own):
-        for s in range(NSLOT):
-            g = jnp.dot(weights[b, rows_of(s), :], rows_in[b], preferred_element_type=F32)
-            if s == 0:
-                own[b] = g
-            else:
-                parts[b * KSLOTS + s - 1] = g.astype(BF16)
+        g = jnp.dot(weights[b], rows_in[b], preferred_element_type=F32)
+        own[b] = g[:BLOCK]
+        for s in range(KSLOTS):
+            parts[b * KSLOTS + s] = g[(s + 1) * BLOCK:(s + 2) * BLOCK].astype(BF16)
 
     def query_side(b, pair):
         cols = pl.ds(pair * 2 * BLOCK, 2 * BLOCK)
         o2 = o_st[b, cols, :]
+        dp_s[...] = lax.dot_general(v_s[b], o2, NT, preferred_element_type=F32)
         out_t = jnp.dot(vt_s[b], p_s[b, :, cols], preferred_element_type=F32)
         att_t = out_t.astype(BF16)
         delta = jnp.sum(o2.T.astype(F32) * att_t.astype(F32), axis=0, keepdims=True)
         inv = inv_s[b, pl.ds(0, 1), cols] * SCALING
         for s in range(NSLOT):
-            dp = lax.dot_general(v_s[b, rows_of(s), :], o2, NT, preferred_element_type=F32)
+            dp = dp_s[rows_of(s), :]
             ds_s[b, rows_of(s), cols] = ((e_s[b, rows_of(s), cols] * inv) * (dp - delta)).astype(BF16)
         gq_t = jnp.dot(kt_s[b], ds_s[b, :, cols], preferred_element_type=F32).astype(BF16)
         att, gq = att_t.T, gq_t.T
@@ -288,11 +264,8 @@
                 stage[2 + i, (dx - 1) * ZN + j] = parts[i][slot_s[dx * ZN + RANGE_AT[j]]]
         moves[2 + i][t] = spread(2 + i, GROUPS[t], terms.at[i])
 
-    def scatter_on(i, t):
-        passed[2 + i][t] = forward(2 + i, GROUPS[t], moves[2 + i][t], terms.at[i])
-
     def row_sums(i, t):
-        arrive(moves[2 + i][t], passed[2 + i][t])
+        arrive(moves[2 + i][t])
         first, count = GROUPS[t]
         for j in range(first, first + count):
             u = RANGE_AT[j]
@@ -312,62 +285,67 @@
             rowsum[i, u, 0] = low.astype(BF16)
             rowsum[i, u, 1] = high.astype(BF16)
 
-    chains = [None, None]
+    chains = [{}, {}]
 
     def chain(i, t):
-        out = []
         for j, d in enumerate((1, -1)):
             u = (-d * t) % ZN
-            half = pl.ds(0 if d == 1 else 1, 1)
-            if t == top:
-                src, dst = rowsum.at[i, u, half], ring.at[i, j, t - 1, half]
-            else:
-                chains[i][j].wait_recv()
+            dst = ring.at[i, j, t - 1]
+            src = rowsum.at[i, u]
+            if t == 4:
+                src, dst = src.at[pl.ds(j, 1)], dst.at[pl.ds(j, 1)]
+            if t == 2:
+                chains[i][3, d].wait_recv()
+                chains[i][4, d].wait_recv()
                 for w in range(BLK_DEV):
-                    if t + 1 < top or w == j:
-                        both = rowsum[i, u, w].astype(F32) + ring[i, j, t, w].astype(F32)
-                        rowsum[i, u, w] = both.astype(BF16)
-                src, dst = rowsum.at[i, u], ring.at[i, j, t - 1]
-            out.append(send(src, dst, along_z(-d)))
-        chains[i] = out
+                    both = rowsum[i, u, w].astype(F32) + ring[i, j, 2, w].astype(F32)
+                    if w == j:
+                        both = both + ring[i, j, 3, w].astype(F32)
+                    rowsum[i, u, w] = both.astype(BF16)
+            chains[i][t, d] = send(src, dst, along_z(-d * t if t < 3 else (2 - t) * d))
 
     def finish(i):
-        for copy in chains[i]:
-            copy.wait_recv()
+        for t in (1, 2):
+            for d in (1, -1):
+                chains[i][t, d].wait_recv()
         own = (own_k, own_v)[i]
         out = (outk_ref, outv_ref)[i]
         for w in range(BLK_DEV):
             total = own[w] + rowsum[i, 0, w].astype(F32)
-            total = total + ring[i, 0, 0, w].astype(F32) + ring[i, 1, 0, w].astype(F32)
+            for t in (1, 2):
+                for j in (0, 1):
+                    total = total + ring[i, j, t - 1, w].astype(F32)
             out[w] = total.astype(BF16)
 
     pairs = GROUP // 2
     units = [(b, pair) for b in range(BLK_DEV) for pair in range(pairs)]
     for i in (0, 1):
         parts[i][ENTRIES] = jnp.zeros((BLOCK, DH), BF16)
-    for n, (b, pair) in enumerate(units):
+    for b, pair in units:
         if pair == 0:
             fetch(0, b)
         probs(b, pair)
-        if n <= top:
-            gather_on(1, n)
         if pair == pairs - 1:
             key_side(b, p_s, o_st, parts_v, own_v)
     for t in range(top, -1, -1):
         scatter_x(1, t)
     for t in range(top + 1):
-        arrive(moves[1][t], passed[1][t])
+        arrive(moves[1][t])
     stores = []
+
+    def sums_on(i, t):
+        row_sums(i, t)
+        if t in (4, 3, 1):
+            chain(i, t)
+        if t == 1:
+            chain(i, 2)
+
     for n, (b, pair) in enumerate(units):
         if pair == 0:
             fetch(1, b)
         query_side(b, pair)
-        if n <= top:
-            scatter_on(1, top - n)
         if n > 2:
-            row_sums(1, top + 3 - n)
-            if n - 3 < top:
-                chain(1, top + 3 - n)
+            sums_on(1, top + 3 - n)
         if pair == pairs - 1:
             key_side(b, ds_s, q_st, parts_k, own_k)
             for src, dst in ((att_s, att_hbm), (gq_s, gq_hbm)):
@@ -376,18 +354,8 @@
                 stores.append(copy)
     for t in range(top, -1, -1):
         scatter_x(0, t)
-    done = len(units) - 3
     for t in range(top, -1, -1):
-        scatter_on(0, t)
-        if top - t >= done:
-            row_sums(1, t)
-    for t in range(top - done, -1, -1):
-        if t > 0 and top - t >= done:
-            chain(1, t)
-    for t in range(top, -1, -1):
-        row_sums(0, t)
-        if t > 0:
-            chain(0, t)
+        sums_on(0, t)
     finish(1)
     finish(0)
     for copy in sent:
@@ -412,7 +380,7 @@
         scratch_shapes=[
             vmem(wide, BF16), vmem(wide, BF16), vmem(wide, BF16), vmem(wide, BF16),
             vmem((FAR + BLK_DEV * ZN, BLOCK, DH), BF16), vmem((FAR + BLK_DEV * ZN, BLOCK, DH), BF16),
-            vmem((4, FAR, BLOCK, DH), BF16), vmem((4, 2, ZN, HALF, DH), BF16), vmem((2, FAR, BLOCK, DH), BF16),
+            vmem((4, FAR, BLOCK, DH), BF16), vmem((2, FAR, BLOCK, DH), BF16),
             vmem((2, 2, ZN // 2, BLK_DEV, BLOCK, DH), BF16), vmem((2, ZN, BLK_DEV, BLOCK, DH), BF16),
             vmem((ENTRIES + 1, BLOCK, DH), BF16), vmem((ENTRIES + 1, BLOCK, DH), BF16),
             vmem(own, F32), vmem(own, F32),
@@ -421,7 +389,7 @@
             vmem((BLK_DEV, GROUP * BLOCK, DH), BF16), vmem((BLK_DEV, GROUP * BLOCK, DH), BF16),
             vmem((BLK_DEV, WIDE, GROUP * BLOCK), F32),
             vmem((BLK_DEV, WIDE, GROUP * BLOCK), BF16), vmem((BLK_DEV, WIDE, GROUP * BLOCK), BF16),
-            vmem((BLK_DEV, 8, GROUP * BLOCK), F32),
+            vmem((WIDE, 2 * BLOCK), F32), vmem((BLK_DEV, 8, GROUP * BLOCK), F32),
             pltpu.SMEM((XN * ZN,), jnp.int32), pltpu.SMEM((XN * ZN,), jnp.int32), pltpu.SMEM((ENTRIES,), jnp.int32),
             pltpu.SemaphoreType.DMA((COPIES,)), pltpu.SemaphoreType.DMA((COPIES,)), pltpu.SemaphoreType.DMA((8,))],
         compiler_params=pltpu.CompilerParams(collective_id=0, has_side_effects=True, vmem_limit_bytes=56 << 20),

time: 94.3 us -> 74.9 us (0.79)
  Pallas kernels: 87.7 us -> 68.3 us
    pallas_call x1, Pallas kernels: 87.7 us -> 68.3 us  [local(): pl.pallas_call(kernel, out_shape=[jax.ShapeDtypeStruct(wide, BF16)] * 2 +...]
where the time goes in v4:
time: 74.9 us; the launch traced here: 74.6 us
  Pallas kernels  68.3 us (91%)
  local copies, waits for them, and re-layouts  5.67 us (8%)
    pallas_call x1, Pallas kernels, local(): pl.pallas_call(kernel, out_shape=[jax.ShapeDtypeStruct(wide, BF16)] * 2 +...  68.3 us
    unnamed x13, local copies, waits for them, and re-layouts  5.67 us

profile of v4, /device:TPU:8, one launch (start us, length us, event | category | flops | bytes accessed | tf_op | source)
XLA Modules:
  0.0 74.6 jit_solution(15421160547743525990)
XLA Ops:
  0.6 0.0 copy-start.3
  0.6 0.7 copy-done.3
  1.3 0.7 copy.10.kb
  2.0 68.3 %sparse_attention.1 = (bf16[2,128,1024]{2,1,0:T(8,128)(2,1)}, bf16[2,128,1024]{2,1,0:T(8,128)(2,1)}, bf16[2,128,128]{2,1,0:T(8,128)(2,1)}, bf16[2,128,128]{2,1,0:T(8,128)(2,1)}) custom-call(s32[64,6]{1,0:T(8,128)} %copy.10.kb, s32[64]{0:T(128)} %kc.1, bf16[2,128,1024]{2,1,0:T(8,128)(2,1)} %bitcast.8, bf16[2,128,1024]{2,1,0:T(8,128)(2,1)} %bitcast.9, ...), custom_call_target="tpu_custom_call" | custom-call | tf_op jit(solution)/shard_map/sparse_attention/pallas_call | solution.py:375
  70.3 0.0 copy-start
  70.3 1.9 %copy.15 = bf16[256,1024]{1,0:T(8,128)(2,1)} copy(bf16[256,1024]{1,0:T(8,128)(2,1)} %bitcast.11) | data formatting | bytes 1048576
  72.2 0.0 copy-done
  72.2 0.0 copy-start.2
  72.2 0.8 %copy.16 = bf16[256,1024]{1,0:T(8,128)(2,1)} copy(bf16[256,1024]{1,0:T(8,128)(2,1)S(1)} %bitcast.10) | data formatting | bytes 1048576
  73.0 0.1 copy-done.2
  73.1 0.0 copy-start.1
  73.1 0.6 copy.17
  73.7 0.2 copy-done.1
  74.0 0.6 copy.18
Async XLA Ops:
  0.6 0.7 copy-start.3
  70.3 1.9 %copy-start = (bf16[2,128,1024]{2,1,0:T(8,128)(2,1)S(1)}, bf16[2,128,1024]{2,1,0:T(8,128)(2,1)}, u32[]{:S(2)}) copy-start(bf16[2,128,1024]{2,1,0:T(8,128)(2,1)} %get-tuple-element.9) | copy-start | bytes 1572868
  72.2 0.9 %copy-start.2 = (bf16[2,128,128]{2,1,0:T(8,128)(2,1)S(1)}, bf16[2,128,128]{2,1,0:T(8,128)(2,1)}, u32[]{:S(2)}) copy-start(bf16[2,128,128]{2,1,0:T(8,128)(2,1)} %get-tuple-element.10) | copy-start | bytes 196612
  73.1 0.9 %copy-start.1 = (bf16[2,128,128]{2,1,0:T(8,128)(2,1)S(1)}, bf16[2,128,128]{2,1,0:T(8,128)(2,1)}, u32[]{:S(2)}) copy-start(bf16[2,128,128]{2,1,0:T(8,128)(2,1)} %get-tuple-element.11) | copy-start | bytes 196612

commit v5 on v4

--- a/solution.py
+++ b/solution.py
@@ -24,7 +24,8 @@
 SCALING = 1.0 / math.sqrt(DH)
 SCALE2 = SCALING * 1.4426950408889634
 NEG = -1e30
-COPIES = 160
+SENDS = 8
+RECVS = 44
 MESH = pl.DeviceIdType.MESH
 BF16 = jnp.bfloat16
 F32 = jnp.float32
@@ -72,7 +73,7 @@
         reader = along_x(dx) * BLK_DEV
         blocks, owners = [], []
         for e in range(ENTRIES):
-            block = kb[reader + e // KSLOTS, e % KSLOTS]
+            block = kb[e % KSLOTS, reader + e // KSLOTS]
             live = e % KSLOTS < kc[reader + e // KSLOTS]
             blocks.append(lax.rem(block, BLK_DEV))
             owners.append(jnp.where(live, lax.div(block, BLK_DEV), -1))
@@ -94,7 +95,7 @@
         block = position * BLK_DEV + b
         first = None
         for s in range(KSLOTS):
-            listed = kb[block, s]
+            listed = kb[s, block]
             owner = lax.div(listed, BLK_DEV)
             dx = lax.rem(lax.rem(owner, XN) - x + XN, XN)
             u = lax.rem(lax.div(owner, XN) - z + ZN, ZN)
@@ -104,17 +105,27 @@
             load_s[b * KSLOTS + s] = jnp.where(s < kc[block], at, first)
 
     used = [0]
-    sent = []
-
-    def send(src, dst, device):
-        at = used[0]
+
+    def fresh():
         used[0] += 1
+        return used[0] - 1
+
+    def send(src, dst, device, out, at):
         copy = pltpu.make_async_remote_copy(
-            src_ref=src, dst_ref=dst, send_sem=send_sem.at[at], recv_sem=recv_sem.at[at],
+            src_ref=src, dst_ref=dst, send_sem=send_sem.at[out], recv_sem=recv_sem.at[at],
             device_id={"ctx": device}, device_id_type=MESH)
         copy.start()
-        sent.append(copy)
         return copy
+
+    def wait_sent(ref, out):
+        pltpu.make_async_remote_copy(
+            src_ref=ref, dst_ref=ref, send_sem=send_sem.at[out], recv_sem=recv_sem.at[0],
+            device_id={"ctx": partners[0]}, device_id_type=MESH).wait_send()
+
+    def wait_come(ref, at):
+        pltpu.make_async_remote_copy(
+            src_ref=ref, dst_ref=ref, send_sem=send_sem.at[0], recv_sem=recv_sem.at[at],
+            device_id={"ctx": partners[0]}, device_id_type=MESH).wait_recv()
 
     def column(i, u, half=None):
         first = FAR + BLK_DEV * (u % ZN)
@@ -123,22 +134,18 @@
         return near[i].at[pl.ds(first + half, 1)]
 
     def ring_near(i):
-        return {(t, d): send(kv_hbm[i], column(i, -d * t), along_z(d * t)) for t in (1, 2) for d in (1, -1)}
+        return {(t, d): send(kv_hbm[i], column(i, -d * t), along_z(d * t), i, fresh()) for t in (1, 2) for d in (1, -1)}
 
     def ring_far(i):
-        out = {(3, d): send(column(i, -2 * d), column(i, -3 * d), along_z(d)) for d in (1, -1)}
+        out = {(3, d): send(column(i, -2 * d), column(i, -3 * d), along_z(d), i, fresh()) for d in (1, -1)}
         for half, d in enumerate((1, -1)):
-            out[4, d] = send(column(i, -2 * d, half), column(i, 4, half), along_z(2 * d))
+            out[4, d] = send(column(i, -2 * d, half), column(i, 4, half), along_z(2 * d), i, fresh())
         return out
 
-    def spread(phase, group, dst):
+    def spread(phase, group, dst_at, at):
         first, count = group
-        return [send(stage.at[phase, pl.ds((dx - 1) * ZN + first, count)],
-                     dst.at[pl.ds((XN - dx - 1) * ZN + first, count)], along_x(dx)) for dx in (2, 1, 3)]
-
-    def arrive(copies):
-        for copy in copies:
-            copy.wait_recv()
+        for dx in (2, 1, 3):
+            send(stage.at[phase, pl.ds((dx - 1) * ZN + first, count)], dst_at(XN - dx, first, count), along_x(dx), 4 + phase, at)
 
     def choose(i, group):
         first, count = group
@@ -151,12 +158,12 @@
     pl.semaphore_wait(barrier, len(partners))
 
     top = ZN // 2
-    moves = [[None] * len(GROUPS) for _ in range(4)]
+    far_come = [fresh(), fresh()]
     rings = [{}, {}]
 
     def gather_x(i, t):
         choose(i, GROUPS[t])
-        moves[i][t] = spread(i, GROUPS[t], near[i])
+        spread(i, GROUPS[t], lambda dx, first, count: near[i].at[pl.ds((dx - 1) * ZN + first, count)], far_come[i])
 
     def come(i, t):
         for d in (1, -1):
@@ -188,8 +195,7 @@
     gather_x(1, 4)
     loads[2].wait()
     loads[3].wait()
-    for t in range(top + 1):
-        arrive(moves[0][t])
+    wait_come(near[0].at[pl.ds(0, FAR)], far_come[0])
 
     def rows_of(s):
         return pl.ds(s * BLOCK, BLOCK)
@@ -257,16 +263,19 @@
 
     parts = [parts_k, parts_v]
 
+    terms_come = {}
+
     def scatter_x(i, t):
         first, count = GROUPS[t]
         for j in range(first, first + count):
             for dx in range(1, XN):
                 stage[2 + i, (dx - 1) * ZN + j] = parts[i][slot_s[dx * ZN + RANGE_AT[j]]]
-        moves[2 + i][t] = spread(2 + i, GROUPS[t], terms.at[i])
+        terms_come[i, t] = fresh()
+        spread(2 + i, GROUPS[t], lambda dx, first, count: terms.at[i, pl.ds(first, count), dx - 1], terms_come[i, t])
 
     def row_sums(i, t):
-        arrive(moves[2 + i][t])
         first, count = GROUPS[t]
+        wait_come(terms.at[i, pl.ds(first, count)], terms_come[i, t])
         for j in range(first, first + count):
             u = RANGE_AT[j]
             low = high = None
@@ -276,7 +285,7 @@
                 if dx == 0:
                     term = parts[i][slot_s[u]].astype(F32)
                 else:
-                    term = terms[i, (dx - 1) * ZN + j].astype(F32)
+                    term = terms[i, j, dx - 1].astype(F32)
                 second = which_s[dx * ZN + u] == 1
                 up = jnp.where(second, term, 0.0)
                 down = jnp.where(second, 0.0, term)
@@ -302,7 +311,7 @@
                     if w == j:
                         both = both + ring[i, j, 3, w].astype(F32)
                     rowsum[i, u, w] = both.astype(BF16)
-            chains[i][t, d] = send(src, dst, along_z(-d * t if t < 3 else (2 - t) * d))
+            chains[i][t, d] = send(src, dst, along_z(-d * t if t < 3 else (2 - t) * d), 2 + i, fresh())
 
     def finish(i):
         for t in (1, 2):
@@ -329,8 +338,7 @@
             key_side(b, p_s, o_st, parts_v, own_v)
     for t in range(top, -1, -1):
         scatter_x(1, t)
-    for t in range(top + 1):
-        arrive(moves[1][t])
+    wait_come(near[1].at[pl.ds(0, FAR)], far_come[1])
     stores = []
 
     def sums_on(i, t):
@@ -358,9 +366,27 @@
         sums_on(0, t)
     finish(1)
     finish(0)
-    for copy in sent:
-        copy.wait_send()
+    for i in (0, 1):
+        ring_bytes = near[i].at[pl.ds(0, 7 * BLK_DEV)]
+        wait_sent(ring_bytes, i)
+        wait_sent(ring_bytes, 2 + i)
+    for phase in range(4):
+        wait_sent(stage.at[phase], 4 + phase)
     for copy in stores:
+        copy.wait()
+
+
+def hand_on(*refs):
+    inputs, outputs, held, sems = refs[:4], refs[4:8], refs[8:12], refs[12]
+    parts = [(i, pl.ds(p * BLOCK, BLOCK)) for i in range(4) for p in range(BLK_DEV)]
+    reads = [pltpu.make_async_copy(inputs[i].at[rows], held[i].at[rows], sems.at[0, n]) for n, (i, rows) in enumerate(parts)]
+    writes = [pltpu.make_async_copy(held[i].at[rows], outputs[i].at[rows], sems.at[1, n]) for n, (i, rows) in enumerate(parts)]
+    for copy in reads:
+        copy.start()
+    for read, write in zip(reads, writes):
+        read.wait()
+        write.start()
+    for copy in writes:
         copy.wait()
 
 
@@ -380,7 +406,7 @@
         scratch_shapes=[
             vmem(wide, BF16), vmem(wide, BF16), vmem(wide, BF16), vmem(wide, BF16),
             vmem((FAR + BLK_DEV * ZN, BLOCK, DH), BF16), vmem((FAR + BLK_DEV * ZN, BLOCK, DH), BF16),
-            vmem((4, FAR, BLOCK, DH), BF16), vmem((2, FAR, BLOCK, DH), BF16),
+            vmem((4, FAR, BLOCK, DH), BF16), vmem((2, ZN, XN - 1, BLOCK, DH), BF16),
             vmem((2, 2, ZN // 2, BLK_DEV, BLOCK, DH), BF16), vmem((2, ZN, BLK_DEV, BLOCK, DH), BF16),
             vmem((ENTRIES + 1, BLOCK, DH), BF16), vmem((ENTRIES + 1, BLOCK, DH), BF16),
             vmem(own, F32), vmem(own, F32),
@@ -391,11 +417,19 @@
             vmem((BLK_DEV, WIDE, GROUP * BLOCK), BF16), vmem((BLK_DEV, WIDE, GROUP * BLOCK), BF16),
             vmem((WIDE, 2 * BLOCK), F32), vmem((BLK_DEV, 8, GROUP * BLOCK), F32),
             pltpu.SMEM((XN * ZN,), jnp.int32), pltpu.SMEM((XN * ZN,), jnp.int32), pltpu.SMEM((ENTRIES,), jnp.int32),
-            pltpu.SemaphoreType.DMA((COPIES,)), pltpu.SemaphoreType.DMA((COPIES,)), pltpu.SemaphoreType.DMA((8,))],
+            pltpu.SemaphoreType.DMA((SENDS,)), pltpu.SemaphoreType.DMA((RECVS,)), pltpu.SemaphoreType.DMA((8,))],
         compiler_params=pltpu.CompilerParams(collective_id=0, has_side_effects=True, vmem_limit_bytes=56 << 20),
         name="sparse_attention",
-    )(key_blocks, key_count, queries.reshape(wide), grad_out.reshape(wide), keys.reshape(own), values.reshape(own))
-    return att.reshape(rows, width), gq.reshape(rows, width), gk.reshape(rows, DH), gv.reshape(rows, DH)
+    )(key_blocks.T, key_count, queries.reshape(wide), grad_out.reshape(wide), keys.reshape(own), values.reshape(own))
+    results = [att.reshape(rows, width), gq.reshape(rows, width), gk.reshape(rows, DH), gv.reshape(rows, DH)]
+    return tuple(pl.pallas_call(
+        hand_on,
+        out_shape=[jax.ShapeDtypeStruct(a.shape, a.dtype) for a in results],
+        in_specs=[any_spec] * 4,
+        out_specs=[any_spec] * 4,
+        scratch_shapes=[vmem(a.shape, a.dtype) for a in results] + [pltpu.SemaphoreType.DMA((2, 4 * BLK_DEV))],
+        name="hand_on",
+    )(*results))
 
 
 def solution(mesh):

time: 74.9 us -> 68.3 us (0.912)
  local copies, waits for them, and re-layouts: 5.67 us -> 0 us
  Pallas kernels: 68.3 us -> 67.5 us
    unnamed x13 -> x0, local copies, waits for them, and re-layouts: 5.67 us -> none
    pallas_call x1, Pallas kernels: 68.3 us -> 65.4 us  [local(): pl.pallas_call(kernel, out_shape=[jax.ShapeDtypeStruct(wide, BF16)] * 2 +...]
    pallas_call x0 -> x1, Pallas kernels: none -> 2.08 us  [local(): pl.pallas_call(hand_on, out_shape=[jax.ShapeDtypeStruct(a.shape, a.dtype)...]
where the time goes in v5:
time: 68.3 us; the launch traced here: 68.1 us
  Pallas kernels  67.5 us (99%)
    pallas_call x1, Pallas kernels, local(): pl.pallas_call(kernel, out_shape=[jax.ShapeDtypeStruct(wide, BF16)] * 2 +...  65.4 us
    pallas_call x1, Pallas kernels, local(): pl.pallas_call(hand_on, out_shape=[jax.ShapeDtypeStruct(a.shape, a.dtype)...  2.08 us

profile of v5, /device:TPU:8, one launch (start us, length us, event | category | flops | bytes accessed | tf_op | source)
XLA Modules:
  0.0 68.1 jit_solution(8495741763322805283)
XLA Ops:
  0.6 65.4 %sparse_attention.1 = (bf16[2,128,1024]{2,1,0:T(8,128)(2,1)}, bf16[2,128,1024]{2,1,0:T(8,128)(2,1)}, bf16[2,128,128]{2,1,0:T(8,128)(2,1)}, bf16[2,128,128]{2,1,0:T(8,128)(2,1)}) custom-call(s32[6,64]{1,0:T(8,128)} %bitcast.17, s32[64]{0:T(128)} %kc.1, bf16[2,128,1024]{2,1,0:T(8,128)(2,1)} %bitcast.9, bf16[2,128,1024]{2,1,0:T(8,128)(2,1)} %bitcast.10, ...), custom_call_target="tpu_custom_call" | custom-call | tf_op jit(solution)/shard_map/sparse_attention/pallas_call | solution.py:401
  66.0 2.1 %hand_on.1 = (bf16[256,1024]{1,0:T(8,128)(2,1)}, bf16[256,1024]{1,0:T(8,128)(2,1)}, bf16[256,128]{1,0:T(8,128)(2,1)}, bf16[256,128]{1,0:T(8,128)(2,1)}) custom-call(bf16[256,1024]{1,0:T(8,128)(2,1)} %bitcast.11, bf16[256,1024]{1,0:T(8,128)(2,1)} %bitcast.12, bf16[256,128]{1,0:T(8,128)(2,1)} %bitcast.15, bf16[256,128]{1,0:T(8,128)(2,1)} %bitcast.16), custom_call_target="tpu_custom_call" | custom-call | tf_op jit(solution)/shard_map/hand_on/pallas_call | solution.py:425

commit v6 on v5

--- a/solution.py
+++ b/solution.py
@@ -24,8 +24,10 @@
 SCALING = 1.0 / math.sqrt(DH)
 SCALE2 = SCALING * 1.4426950408889634
 NEG = -1e30
-SENDS = 8
-RECVS = 44
+SENDS = 20
+RECVS = 64
+CUT = 80
+REST = BLOCK - CUT
 MESH = pl.DeviceIdType.MESH
 BF16 = jnp.bfloat16
 F32 = jnp.float32
@@ -36,14 +38,18 @@
     return 0 if u == 0 else (2 * u - 1 if u <= ZN // 2 else 2 * (ZN - u))
 
 
+def base(dx):
+    return (dx - 1) * 2 * ZN % FAR
+
+
 GROUPS = [(0, 1)] + [(2 * t - 1, 2) for t in range(1, ZN // 2)] + [(ZN - 1, 1)]
 RANGE_AT = sorted(range(ZN), key=place)
 
 
 def kernel(kb, kc, q_hbm, o_hbm, k_hbm, v_hbm, att_hbm, gq_hbm, outk_ref, outv_ref,
-           q_in, o_in, att_s, gq_s, near_k, near_v, stage, terms, ring, rowsum,
+           q_in, o_in, att_s, gq_s, near_k, near_v, stage, other, beyond, terms, terms_far, other_terms, other_sum, other_in, ring, rowsum,
            parts_k, parts_v, own_k, own_v, k_s, v_s, kt_s, vt_s, q_st, o_st, e_s, p_s, ds_s, dp_s, inv_s,
-           which_s, slot_s, load_s, send_sem, recv_sem, local_sem):
+           which_s, slot_s, other_s, load_s, send_sem, recv_sem, local_sem):
     position = lax.axis_index("ctx")
     x = lax.rem(position, XN)
     z = lax.div(position, XN)
@@ -57,7 +63,7 @@
         return lax.rem(z + dz % ZN, ZN) * XN + x
 
     barrier = pltpu.get_barrier_semaphore()
-    partners = [along_x(d) for d in range(1, XN)] + [along_z(d) for d in (1, -1, 2, -2)]
+    partners = [along_x(d) for d in range(1, XN)] + [along_z(u) for u in range(1, ZN)]
     for partner in partners:
         pl.semaphore_signal(barrier, inc=1, device_id={"ctx": partner}, device_id_type=MESH)
 
@@ -91,6 +97,14 @@
                     for e in range(ENTRIES):
                         slot = jnp.where(owners[e] == wanted, e, slot)
                     slot_s[ax * ZN + u] = slot
+    for u in range(ZN):
+        reader = along_z(u) * BLK_DEV
+        which = jnp.int32(0)
+        for e in range(ENTRIES):
+            block = kb[e % KSLOTS, reader + e // KSLOTS]
+            hit = (e % KSLOTS < kc[reader + e // KSLOTS]) & (lax.div(block, BLK_DEV) == along_x(2))
+            which = jnp.where(hit, lax.rem(block, BLK_DEV), which)
+        other_s[u] = which
     for b in range(BLK_DEV):
         block = position * BLK_DEV + b
         first = None
@@ -100,7 +114,7 @@
             dx = lax.rem(lax.rem(owner, XN) - x + XN, XN)
             u = lax.rem(lax.div(owner, XN) - z + ZN, ZN)
             spot = jnp.where(u == 0, 0, jnp.where(u <= ZN // 2, 2 * u - 1, 2 * (ZN - u)))
-            at = jnp.where(dx == 0, FAR + BLK_DEV * u + lax.rem(listed, BLK_DEV), (dx - 1) * ZN + spot)
+            at = jnp.where(dx == 0, FAR + BLK_DEV * u + lax.rem(listed, BLK_DEV), lax.rem((dx + 2) * 2 * ZN, FAR) + spot)
             first = at if s == 0 else first
             load_s[b * KSLOTS + s] = jnp.where(s < kc[block], at, first)
 
@@ -134,7 +148,10 @@
         return near[i].at[pl.ds(first + half, 1)]
 
     def ring_near(i):
-        return {(t, d): send(kv_hbm[i], column(i, -d * t), along_z(d * t), i, fresh()) for t in (1, 2) for d in (1, -1)}
+        return {(1, d): send(kv_hbm[i], column(i, -d), along_z(d), i, fresh()) for d in (1, -1)}
+
+    def ring_mid(i):
+        return {(2, d): send(column(i, -d), column(i, -2 * d), along_z(d), i, fresh()) for d in (1, -1)}
 
     def ring_far(i):
         out = {(3, d): send(column(i, -2 * d), column(i, -3 * d), along_z(d), i, fresh()) for d in (1, -1)}
@@ -142,10 +159,29 @@
             out[4, d] = send(column(i, -2 * d, half), column(i, 4, half), along_z(2 * d), i, fresh())
         return out
 
-    def spread(phase, group, dst_at, at):
+    def spread(phase, group, dst_at, at, at_far):
         first, count = group
-        for dx in (2, 1, 3):
-            send(stage.at[phase, pl.ds((dx - 1) * ZN + first, count)], dst_at(XN - dx, first, count), along_x(dx), 4 + phase, at)
+        rows = pl.ds(0, CUT)
+        send(stage.at[phase, pl.ds(base(2) + first, count), rows], dst_at(2, first, count), along_x(2), 8 + phase, at_far)
+        for dx in (1, 3):
+            send(stage.at[phase, pl.ds(base(dx) + first, count)], dst_at(XN - dx, first, count), along_x(dx), 4 + phase, at)
+
+    def cross(i):
+        return send(kv_hbm[i].at[:, pl.ds(CUT, REST)], other.at[i], along_x(2), 16 + i, fresh())
+
+    def cross_on(i):
+        crossing[i].wait_recv()
+        rows = pl.ds(CUT, REST)
+        low, high = other[i, 0], other[i, 1]
+        for u in range(1, ZN):
+            beyond[i, u] = jnp.where(other_s[u] == 1, high, low)
+            send(beyond.at[i, u], near[i].at[base(2) + place(-u % ZN), rows], along_z(u), 12 + i, beyond_come[i])
+        near[i][base(2), CUT:] = jnp.where(other_s[0] == 1, high, low)
+
+    def all_come(i):
+        wait_come(near[i].at[pl.ds(0, 2 * ZN)], far_come[i])
+        wait_come(near[i].at[pl.ds(2 * ZN, ZN), pl.ds(0, CUT)], opposite_come[i])
+        wait_come(near[i].at[pl.ds(2 * ZN + 1, ZN - 1), pl.ds(CUT, REST)], beyond_come[i])
 
     def choose(i, group):
         first, count = group
@@ -153,35 +189,48 @@
             u = RANGE_AT[j]
             low, high = near[i][FAR + BLK_DEV * u], near[i][FAR + BLK_DEV * u + 1]
             for dx in range(1, XN):
-                stage[i, (dx - 1) * ZN + j] = jnp.where(which_s[dx * ZN + u] == 1, high, low)
+                stage[i, base(dx) + j] = jnp.where(which_s[dx * ZN + u] == 1, high, low)
 
     pl.semaphore_wait(barrier, len(partners))
 
     top = ZN // 2
     far_come = [fresh(), fresh()]
+    opposite_come = [fresh(), fresh()]
+    beyond_come = [fresh(), fresh()]
+    crossing = [None, None]
     rings = [{}, {}]
 
     def gather_x(i, t):
         choose(i, GROUPS[t])
-        spread(i, GROUPS[t], lambda dx, first, count: near[i].at[pl.ds((dx - 1) * ZN + first, count)], far_come[i])
+        def at(dx, first, count):
+            slots = pl.ds(base(dx) + first, count)
+            return near[i].at[slots] if dx != 2 else near[i].at[slots, pl.ds(0, CUT)]
+
+        spread(i, GROUPS[t], at, far_come[i], opposite_come[i])
 
     def come(i, t):
         for d in (1, -1):
             rings[i][t, d].wait_recv()
 
     rings[0].update(ring_near(0))
+    crossing[0] = cross(0)
     loads[0].wait()
     gather_x(0, 0)
     rings[1].update(ring_near(1))
     come(0, 1)
+    rings[0].update(ring_mid(0))
     gather_x(0, 1)
+    crossing[1] = cross(1)
+    cross_on(0)
+    loads[1].wait()
+    gather_x(1, 0)
+    come(1, 1)
+    rings[1].update(ring_mid(1))
     come(0, 2)
     rings[0].update(ring_far(0))
     gather_x(0, 2)
-    loads[1].wait()
-    gather_x(1, 0)
-    come(1, 1)
     gather_x(1, 1)
+    cross_on(1)
     come(1, 2)
     rings[1].update(ring_far(1))
     come(0, 3)
@@ -195,7 +244,7 @@
     gather_x(1, 4)
     loads[2].wait()
     loads[3].wait()
-    wait_come(near[0].at[pl.ds(0, FAR)], far_come[0])
+    all_come(0)
 
     def rows_of(s):
         return pl.ds(s * BLOCK, BLOCK)
@@ -269,30 +318,58 @@
         first, count = GROUPS[t]
         for j in range(first, first + count):
             for dx in range(1, XN):
-                stage[2 + i, (dx - 1) * ZN + j] = parts[i][slot_s[dx * ZN + RANGE_AT[j]]]
-        terms_come[i, t] = fresh()
-        spread(2 + i, GROUPS[t], lambda dx, first, count: terms.at[i, pl.ds(first, count), dx - 1], terms_come[i, t])
+                stage[2 + i, base(dx) + j] = parts[i][slot_s[dx * ZN + RANGE_AT[j]]]
+        terms_come[i, t] = fresh(), fresh()
+
+        def at(dx, first, count):
+            return terms.at[i, pl.ds(first, count), dx // 2] if dx != 2 else terms_far.at[i, pl.ds(first, count)]
+
+        spread(2 + i, GROUPS[t], at, *terms_come[i, t])
+
+    def scatter_cross(i):
+        terms_come[i] = fresh()
+        for u in range(1, ZN):
+            beyond[2 + i, u] = parts[i][slot_s[2 * ZN + u], pl.ds(CUT, REST)]
+            send(beyond.at[2 + i, u], other_terms.at[i, -u % ZN], along_z(u), 14 + i, terms_come[i])
+
+    def cross_sums(i):
+        wait_come(other_terms.at[i, pl.ds(1, ZN - 1)], terms_come[i])
+        low = high = None
+        for u in range(ZN):
+            term = (parts[i][slot_s[2 * ZN], pl.ds(CUT, REST)] if u == 0 else other_terms[i, u]).astype(F32)
+            second = other_s[u] == 1
+            up = jnp.where(second, term, 0.0)
+            down = jnp.where(second, 0.0, term)
+            high = up if high is None else high + up
+            low = down if low is None else low + down
+        other_sum[i, 0] = low.astype(BF16)
+        other_sum[i, 1] = high.astype(BF16)
+        crossing[i] = send(other_sum.at[i], other_in.at[i], along_x(2), 18 + i, fresh())
 
     def row_sums(i, t):
         first, count = GROUPS[t]
-        wait_come(terms.at[i, pl.ds(first, count)], terms_come[i, t])
+        wait_come(terms.at[i, pl.ds(first, count)], terms_come[i, t][0])
+        wait_come(terms_far.at[i, pl.ds(first, count)], terms_come[i, t][1])
         for j in range(first, first + count):
             u = RANGE_AT[j]
-            low = high = None
-            for dx in range(XN):
-                if dx == 0 and u == 0:
-                    continue
-                if dx == 0:
-                    term = parts[i][slot_s[u]].astype(F32)
-                else:
-                    term = terms[i, j, dx - 1].astype(F32)
-                second = which_s[dx * ZN + u] == 1
-                up = jnp.where(second, term, 0.0)
-                down = jnp.where(second, 0.0, term)
-                high = up if high is None else high + up
-                low = down if low is None else low + down
-            rowsum[i, u, 0] = low.astype(BF16)
-            rowsum[i, u, 1] = high.astype(BF16)
+            for start, size in ((0, CUT), (CUT, REST)):
+                rows = pl.ds(start, size)
+                low = high = None
+                for dx in range(XN):
+                    if dx == 0 and u == 0 or dx == 2 and start > 0:
+                        continue
+                    if dx == 0:
+                        term = parts[i][slot_s[u], rows]
+                    else:
+                        term = terms_far[i, j] if dx == 2 else terms[i, j, dx // 2, rows]
+                    term = term.astype(F32)
+                    second = which_s[dx * ZN + u] == 1
+                    up = jnp.where(second, term, 0.0)
+                    down = jnp.where(second, 0.0, term)
+                    high = up if high is None else high + up
+                    low = down if low is None else low + down
+                rowsum[i, u, 0, rows] = low.astype(BF16)
+                rowsum[i, u, 1, rows] = high.astype(BF16)
 
     chains = [{}, {}]
 
@@ -317,6 +394,7 @@
         for t in (1, 2):
             for d in (1, -1):
                 chains[i][t, d].wait_recv()
+        crossing[i].wait_recv()
         own = (own_k, own_v)[i]
         out = (outk_ref, outv_ref)[i]
         for w in range(BLK_DEV):
@@ -324,7 +402,8 @@
             for t in (1, 2):
                 for j in (0, 1):
                     total = total + ring[i, j, t - 1, w].astype(F32)
-            out[w] = total.astype(BF16)
+            out[w, :CUT] = total[:CUT].astype(BF16)
+            out[w, CUT:] = (total[CUT:] + other_in[i, w].astype(F32)).astype(BF16)
 
     pairs = GROUP // 2
     units = [(b, pair) for b in range(BLK_DEV) for pair in range(pairs)]
@@ -336,9 +415,10 @@
         probs(b, pair)
         if pair == pairs - 1:
             key_side(b, p_s, o_st, parts_v, own_v)
+    scatter_cross(1)
     for t in range(top, -1, -1):
         scatter_x(1, t)
-    wait_come(near[1].at[pl.ds(0, FAR)], far_come[1])
+    all_come(1)
     stores = []
 
     def sums_on(i, t):
@@ -352,18 +432,26 @@
         if pair == 0:
             fetch(1, b)
         query_side(b, pair)
-        if n > 2:
-            sums_on(1, top + 3 - n)
+        if n == 5:
+            sums_on(1, 4)
+        if n == 7:
+            sums_on(1, 3)
         if pair == pairs - 1:
             key_side(b, ds_s, q_st, parts_k, own_k)
             for src, dst in ((att_s, att_hbm), (gq_s, gq_hbm)):
                 copy = pltpu.make_async_copy(src.at[b], dst.at[b], local_sem.at[4 + len(stores)])
                 copy.start()
                 stores.append(copy)
+    scatter_cross(0)
     for t in range(top, -1, -1):
         scatter_x(0, t)
+    cross_sums(1)
+    for t in (2, 1, 0):
+        sums_on(1, t)
     for t in range(top, -1, -1):
         sums_on(0, t)
+        if t == 3:
+            cross_sums(0)
     finish(1)
     finish(0)
     for i in (0, 1):
@@ -371,7 +459,12 @@
         wait_sent(ring_bytes, i)
         wait_sent(ring_bytes, 2 + i)
     for phase in range(4):
-        wait_sent(stage.at[phase], 4 + phase)
+        wait_sent(stage.at[phase, pl.ds(0, 2 * ZN)], 4 + phase)
+        wait_sent(stage.at[phase, pl.ds(2 * ZN, ZN), pl.ds(0, CUT)], 8 + phase)
+        wait_sent(beyond.at[phase, pl.ds(1, ZN - 1)], 12 + phase)
+    for i in (0, 1):
+        wait_sent(other.at[i], 16 + i)
+        wait_sent(other_sum.at[i], 18 + i)
     for copy in stores:
         copy.wait()
 
@@ -406,7 +499,10 @@
         scratch_shapes=[
             vmem(wide, BF16), vmem(wide, BF16), vmem(wide, BF16), vmem(wide, BF16),
             vmem((FAR + BLK_DEV * ZN, BLOCK, DH), BF16), vmem((FAR + BLK_DEV * ZN, BLOCK, DH), BF16),
-            vmem((4, FAR, BLOCK, DH), BF16), vmem((2, ZN, XN - 1, BLOCK, DH), BF16),
+            vmem((4, FAR, BLOCK, DH), BF16), vmem((2, BLK_DEV, REST, DH), BF16), vmem((4, ZN, REST, DH), BF16),
+            vmem((2, ZN, 2, BLOCK, DH), BF16), vmem((2, ZN, CUT, DH), BF16),
+            vmem((2, ZN, REST, DH), BF16), vmem((2, BLK_DEV, REST, DH), BF16), vmem((2, BLK_DEV, REST, DH), BF16),
+
             vmem((2, 2, ZN // 2, BLK_DEV, BLOCK, DH), BF16), vmem((2, ZN, BLK_DEV, BLOCK, DH), BF16),
             vmem((ENTRIES + 1, BLOCK, DH), BF16), vmem((ENTRIES + 1, BLOCK, DH), BF16),
             vmem(own, F32), vmem(own, F32),
@@ -416,7 +512,7 @@
             vmem((BLK_DEV, WIDE, GROUP * BLOCK), F32),
             vmem((BLK_DEV, WIDE, GROUP * BLOCK), BF16), vmem((BLK_DEV, WIDE, GROUP * BLOCK), BF16),
             vmem((WIDE, 2 * BLOCK), F32), vmem((BLK_DEV, 8, GROUP * BLOCK), F32),
-            pltpu.SMEM((XN * ZN,), jnp.int32), pltpu.SMEM((XN * ZN,), jnp.int32), pltpu.SMEM((ENTRIES,), jnp.int32),
+            pltpu.SMEM((XN * ZN,), jnp.int32), pltpu.SMEM((XN * ZN,), jnp.int32), pltpu.SMEM((ZN,), jnp.int32), pltpu.SMEM((ENTRIES,), jnp.int32),
             pltpu.SemaphoreType.DMA((SENDS,)), pltpu.SemaphoreType.DMA((RECVS,)), pltpu.SemaphoreType.DMA((8,))],
         compiler_params=pltpu.CompilerParams(collective_id=0, has_side_effects=True, vmem_limit_bytes=56 << 20),
         name="sparse_attention",

time: 68.3 us -> 62.3 us (0.912)
  Pallas kernels: 67.5 us -> 61.5 us
    pallas_call x1, Pallas kernels: 65.4 us -> 59.5 us  [local(): pl.pallas_call(kernel, out_shape=[jax.ShapeDtypeStruct(wide, BF16)] * 2 +...]
where the time goes in v6:
time: 62.3 us; the launch traced here: 62.2 us
  Pallas kernels  61.5 us (99%)
  between operations  0.64 us (1%)
    pallas_call x1, Pallas kernels, local(): pl.pallas_call(kernel, out_shape=[jax.ShapeDtypeStruct(wide, BF16)] * 2 +...  59.5 us
    pallas_call x1, Pallas kernels, local(): pl.pallas_call(hand_on, out_shape=[jax.ShapeDtypeStruct(a.shape, a.dtype)...  2.08 us

profile of v6, /device:TPU:8, one launch (start us, length us, event | category | flops | bytes accessed | tf_op | source)
XLA Modules:
  0.0 62.2 jit_solution(17685996918162670726)
XLA Ops:
  0.6 59.5 %sparse_attention.1 = (bf16[2,128,1024]{2,1,0:T(8,128)(2,1)}, bf16[2,128,1024]{2,1,0:T(8,128)(2,1)}, bf16[2,128,128]{2,1,0:T(8,128)(2,1)}, bf16[2,128,128]{2,1,0:T(8,128)(2,1)}) custom-call(s32[6,64]{1,0:T(8,128)} %bitcast.17, s32[64]{0:T(128)} %kc.1, bf16[2,128,1024]{2,1,0:T(8,128)(2,1)} %bitcast.9, bf16[2,128,1024]{2,1,0:T(8,128)(2,1)} %bitcast.10, ...), custom_call_target="tpu_custom_call" | custom-call | tf_op jit(solution)/shard_map/sparse_attention/pallas_call | solution.py:494
  60.1 2.1 %hand_on.1 = (bf16[256,1024]{1,0:T(8,128)(2,1)}, bf16[256,1024]{1,0:T(8,128)(2,1)}, bf16[256,128]{1,0:T(8,128)(2,1)}, bf16[256,128]{1,0:T(8,128)(2,1)}) custom-call(bf16[256,1024]{1,0:T(8,128)(2,1)} %bitcast.11, bf16[256,1024]{1,0:T(8,128)(2,1)} %bitcast.12, bf16[256,128]{1,0:T(8,128)(2,1)} %bitcast.15, bf16[256,128]{1,0:T(8,128)(2,1)} %bitcast.16), custom_call_target="tpu_custom_call" | custom-call | tf_op jit(solution)/shard_map/hand_on/pallas_call | solution.py:521

commit v7 on v6

--- a/solution.py
+++ b/solution.py
@@ -213,31 +213,31 @@
             rings[i][t, d].wait_recv()
 
     rings[0].update(ring_near(0))
+    rings[1].update(ring_near(1))
     crossing[0] = cross(0)
+    crossing[1] = cross(1)
     loads[0].wait()
     gather_x(0, 0)
-    rings[1].update(ring_near(1))
+    loads[1].wait()
+    gather_x(1, 0)
     come(0, 1)
     rings[0].update(ring_mid(0))
     gather_x(0, 1)
-    crossing[1] = cross(1)
-    cross_on(0)
-    loads[1].wait()
-    gather_x(1, 0)
     come(1, 1)
     rings[1].update(ring_mid(1))
+    gather_x(1, 1)
+    cross_on(0)
     come(0, 2)
     rings[0].update(ring_far(0))
     gather_x(0, 2)
-    gather_x(1, 1)
     cross_on(1)
     come(1, 2)
     rings[1].update(ring_far(1))
+    gather_x(1, 2)
     come(0, 3)
     gather_x(0, 3)
     come(0, 4)
     gather_x(0, 4)
-    gather_x(1, 2)
     come(1, 3)
     gather_x(1, 3)
     come(1, 4)
@@ -415,9 +415,9 @@
         probs(b, pair)
         if pair == pairs - 1:
             key_side(b, p_s, o_st, parts_v, own_v)
-    scatter_cross(1)
     for t in range(top, -1, -1):
         scatter_x(1, t)
+    scatter_cross(1)
     all_come(1)
     stores = []
 
@@ -442,8 +442,10 @@
                 copy = pltpu.make_async_copy(src.at[b], dst.at[b], local_sem.at[4 + len(stores)])
                 copy.start()
                 stores.append(copy)
+    scatter_x(0, 4)
+    scatter_x(0, 3)
     scatter_cross(0)
-    for t in range(top, -1, -1):
+    for t in (2, 1, 0):
         scatter_x(0, t)
     cross_sums(1)
     for t in (2, 1, 0):

time: 62.3 us -> 61.9 us (level)
  no operation moved by 1% of the time
where the time goes in v7:
time: 61.9 us; the launch traced here: 61.7 us
  Pallas kernels  61.1 us (99%)
  between operations  0.64 us (1%)
    pallas_call x1, Pallas kernels, local(): pl.pallas_call(kernel, out_shape=[jax.ShapeDtypeStruct(wide, BF16)] * 2 +...  59 us
    pallas_call x1, Pallas kernels, local(): pl.pallas_call(hand_on, out_shape=[jax.ShapeDtypeStruct(a.shape, a.dtype)...  2.08 us

profile of v7, /device:TPU:8, one launch (start us, length us, event | category | flops | bytes accessed | tf_op | source)
XLA Modules:
  0.0 61.7 jit_solution(10655318338449404058)
XLA Ops:
  0.6 59.0 %sparse_attention.1 = (bf16[2,128,1024]{2,1,0:T(8,128)(2,1)}, bf16[2,128,1024]{2,1,0:T(8,128)(2,1)}, bf16[2,128,128]{2,1,0:T(8,128)(2,1)}, bf16[2,128,128]{2,1,0:T(8,128)(2,1)}) custom-call(s32[6,64]{1,0:T(8,128)} %bitcast.17, s32[64]{0:T(128)} %kc.1, bf16[2,128,1024]{2,1,0:T(8,128)(2,1)} %bitcast.9, bf16[2,128,1024]{2,1,0:T(8,128)(2,1)} %bitcast.10, ...), custom_call_target="tpu_custom_call" | custom-call | tf_op jit(solution)/shard_map/sparse_attention/pallas_call | solution.py:496
  59.6 2.1 %hand_on.1 = (bf16[256,1024]{1,0:T(8,128)(2,1)}, bf16[256,1024]{1,0:T(8,128)(2,1)}, bf16[256,128]{1,0:T(8,128)(2,1)}, bf16[256,128]{1,0:T(8,128)(2,1)}) custom-call(bf16[256,1024]{1,0:T(8,128)(2,1)} %bitcast.11, bf16[256,1024]{1,0:T(8,128)(2,1)} %bitcast.12, bf16[256,128]{1,0:T(8,128)(2,1)} %bitcast.15, bf16[256,128]{1,0:T(8,128)(2,1)} %bitcast.16), custom_call_target="tpu_custom_call" | custom-call | tf_op jit(solution)/shard_map/hand_on/pallas_call | solution.py:523
